TPU v7x, 256 devices: a whole 4x4x8 slice. The times are simulated.
256 devices in a mesh: gx: 8 (over y, core), yz: 32 (over x, z).
Axes of the slice: x: 4, y: 4, z: 8, core: 2. Of those that a mesh axis runs over, the one named last changes fastest.
Arguments:
- guess: float32 [64, 512, 512], P('gx', 'yz'), may hold values from -6 to 6
- rhs: float32 [64, 512, 512], P('gx', 'yz'), may hold values from -6 to 6
- alpha: float32 [64, 512, 512], P('gx', 'yz'), may hold values from 1 to 4
- beta: float32 [64, 512, 512], P('gx', 'yz'), may hold values from 0.25 to 1
Outputs:
- corrected: float32 [64, 512, 512], P('gx', 'yz')
- coarsest_rhs: float32 [16, 128, 128], P(None, 'yz')
All inputs are finite; a program needn't handle non-finite values.
Results may differ from a plain program's by a relative error of at most 0.000068.
Values sent between devices are 32-bit elements; how exact they have to be, the bound alone decides.
A program may use at most 64 MiB of HBM per device.

v0:
```python
import jax
import jax.numpy as jnp
from jax import lax
from jax.sharding import PartitionSpec as P

DEGREE = 4


THETA = 1.125
DELTA = 0.875


def padded_2(cells, sides, width):
    for axis, dim in sides:
        count = lax.axis_size(axis)
        ends = count - 1
        head = lax.slice_in_dim(cells, 0, width, axis=dim)
        tail = lax.slice_in_dim(cells, cells.shape[dim] - width, cells.shape[dim], axis=dim)
        cells = jnp.concatenate(
            [
                lax.ppermute(tail, axis, [(i, (i + 1) % count) for i in range(ends)]),
                cells,
                lax.ppermute(head, axis, [((i + 1) % count, i) for i in range(ends)]),
            ],
            axis=dim,
        )
    return cells


def cheb_terms():
    sigma = THETA / DELTA
    rho_prev = 1.0 / sigma
    terms = []
    for step in range(DEGREE - 1):
        rho_next = 1.0 / (2.0 * sigma - rho_prev)
        terms.append((rho_next * rho_prev, 2.0 * rho_next / DELTA))
        rho_prev = rho_next
    return terms


def pad_fine(field):
    padded = padded_2(field, (("gx", 0), ("yz", 1)), 1)
    return jnp.pad(padded, ((0, 0), (0, 0), (1, 1)))


def pad_split(field):
    padded = padded_2(field, (("gx", 0), ("yz", 1)), 1)
    return jnp.pad(padded, ((0, 0), (0, 0), (1, 1)))


def face_coeffs(beta, padded):
    return (
        0.5 * (beta + padded[2:, 1:-1, 1:-1]),
        0.5 * (beta + padded[:-2, 1:-1, 1:-1]),
        0.5 * (beta + padded[1:-1, 2:, 1:-1]),
        0.5 * (beta + padded[1:-1, :-2, 1:-1]),
        0.5 * (beta + padded[1:-1, 1:-1, 2:]),
        0.5 * (beta + padded[1:-1, 1:-1, :-2]),
    )


def operate(field, padded, alpha, faces, scale):
    terms = faces[0] * (field - padded[2:, 1:-1, 1:-1]) + faces[1] * (
        field - padded[:-2, 1:-1, 1:-1]
    )
    terms = (
        terms
        + faces[2] * (field - padded[1:-1, 2:, 1:-1])
        + faces[3] * (field - padded[1:-1, :-2, 1:-1])
    )
    terms = (
        terms
        + faces[4] * (field - padded[1:-1, 1:-1, 2:])
        + faces[5] * (field - padded[1:-1, 1:-1, :-2])
    )
    return alpha * field + scale * terms


def smooth(start, source, alpha, faces, scale, pad_fn, from_zero, inside=1.0):
    total = faces[0] + faces[1] + faces[2] + faces[3] + faces[4] + faces[5]
    inverse = inside / (alpha + scale * total + (1.0 - inside))
    if from_zero:
        resid = inverse * source
    else:
        resid = inverse * (source - operate(start, pad_fn(start), alpha, faces, scale))
    update = resid * (1.0 / THETA)
    field = start + update
    for first, second in cheb_terms():
        resid = inverse * (source - operate(field, pad_fn(field), alpha, faces, scale))
        update = first * update + second * resid
        field = field + update
    return field


def restrict(field):
    size_a, size_b, size_c = field.shape
    blocks = field.reshape(size_a // 2, 2, size_b // 2, 2, size_c // 2, 2)
    return jnp.sum(blocks, axis=(1, 3, 5)) * 0.125


def prolong(field):
    size_a, size_b, size_c = field.shape
    wide = jnp.broadcast_to(field[:, None, :, None, :, None], (size_a, 2, size_b, 2, size_c, 2))
    return wide.reshape(2 * size_a, 2 * size_b, 2 * size_c)


def on_device(guess, rhs, alpha, beta):
    faces = face_coeffs(beta, pad_fine(beta))
    smoothed = smooth(guess, rhs, alpha, faces, 1.0, pad_fine, False)
    fine_resid = rhs - operate(smoothed, pad_fine(smoothed), alpha, faces, 1.0)
    coarse_rhs = restrict(fine_resid)
    coarse_alpha = restrict(alpha)
    coarse_beta = restrict(beta)
    coarse_faces = face_coeffs(coarse_beta, pad_split(coarse_beta))
    coarse_x = smooth(
        jnp.zeros_like(coarse_rhs), coarse_rhs, coarse_alpha, coarse_faces, 0.25, pad_split, True
    )
    coarse_resid = coarse_rhs - operate(
        coarse_x, pad_split(coarse_x), coarse_alpha, coarse_faces, 0.25
    )
    coarsest = lax.all_gather(restrict(coarse_resid), "gx", axis=0, tiled=True)
    return (smoothed + prolong(coarse_x), coarsest)


def solution(mesh):
    placed = (P("gx", "yz", None), P("gx", "yz", None), P("gx", "yz", None), P("gx", "yz", None))
    return jax.shard_map(
        on_device,
        mesh=mesh,
        in_specs=placed,
        out_specs=(P("gx", "yz", None), P(None, "yz", None)),
        check_vma=False,
    )
```

profile of v0, /device:TPU:7, one launch (start us, length us, event | category | flops | bytes accessed | tf_op | source)
XLA Modules:
  0.0 298.5 jit_solution(12116628224408198905)
XLA Ops:
  9.8 3.6 %collective-permute-start.1 = (f32[1,16,512]{2,1,0:T(8,128)S(1)}, f32[1,16,512]{2,1,0:T(8,128)S(1)}, u32[]{:S(2)}, u32[]{:S(2)}) collective-permute-start(f32[1,16,512]{2,1,0:T(8,128)S(1)} %get-tuple-element.41), channel_id=1, source_target_pairs={{0,32},{32,64},{64,96},{96,128},{128,160},{160,192},{192,224},{1,3... | collective-permute-start | bytes 98312 | tf_op jit(solution)/shard_map/ppermute | solution.py:21
  19.1 6.1 %collective-permute-start.6 = (f32[10,1,512]{2,1,0:T(1,128)S(1)}, f32[10,1,512]{2,1,0:T(1,128)S(1)}, u32[]{:S(2)}, u32[]{:S(2)}) collective-permute-start(f32[10,1,512]{2,1,0:T(1,128)S(1)} %get-tuple-element.31), channel_id=1, source_target_pairs={{1,0},{2,1},{3,2},{4,3},{5,4},{6,5},{7,6},{8,7},{9,8},{10,9},{11,1... | collective-permute-start | bytes 61448 | tf_op jit(solution)/shard_map/ppermute | solution.py:23
  27.2 5.5 %collective-permute-start.2 = (f32[10,1,512]{2,1,0:T(1,128)S(1)}, f32[10,1,512]{2,1,0:T(1,128)S(1)}, u32[]{:S(2)}, u32[]{:S(2)}) collective-permute-start(f32[10,1,512]{2,1,0:T(1,128)S(1)} %get-tuple-element.29), channel_id=1, source_target_pairs={{1,0},{2,1},{3,2},{4,3},{5,4},{6,5},{7,6},{8,7},{9,8},{10,9},{11,1... | collective-permute-start | bytes 61448 | tf_op jit(solution)/shard_map/ppermute | solution.py:23
  36.2 5.6 %collective-permute-start.9 = (f32[1,16,512]{2,1,0:T(8,128)S(1)}, f32[1,16,512]{2,1,0:T(8,128)S(1)}, u32[]{:S(2)}, u32[]{:S(2)}) collective-permute-start(f32[1,16,512]{2,1,0:T(8,128)S(1)} %get-tuple-element.38), channel_id=1, source_target_pairs={{0,32},{32,64},{64,96},{96,128},{128,160},{160,192},{192,224},{1,3... | collective-permute-start | bytes 98312 | tf_op jit(solution)/shard_map/ppermute | solution.py:21
  49.0 6.0 %collective-permute-start.10 = (f32[10,1,512]{2,1,0:T(1,128)S(1)}, f32[10,1,512]{2,1,0:T(1,128)S(1)}, u32[]{:S(2)}, u32[]{:S(2)}) collective-permute-start(f32[10,1,512]{2,1,0:T(1,128)S(1)} %get-tuple-element.27), channel_id=1, source_target_pairs={{1,0},{2,1},{3,2},{4,3},{5,4},{6,5},{7,6},{8,7},{9,8},{10,9},{11,1... | collective-permute-start | bytes 61448 | tf_op jit(solution)/shard_map/ppermute | solution.py:23
  69.2 5.2 %collective-permute-start.14 = (f32[10,1,512]{2,1,0:T(1,128)S(1)}, f32[10,1,512]{2,1,0:T(1,128)S(1)}, u32[]{:S(2)}, u32[]{:S(2)}) collective-permute-start(f32[10,1,512]{2,1,0:T(1,128)S(1)} %get-tuple-element.25), channel_id=1, source_target_pairs={{1,0},{2,1},{3,2},{4,3},{5,4},{6,5},{7,6},{8,7},{9,8},{10,9},{11,1... | collective-permute-start | bytes 61448 | tf_op jit(solution)/shard_map/ppermute | solution.py:23
  74.5 18.8 %reshape.21 = f32[4,2,8,2,256,2]{5,4,3,2,1,0:T(8,128)} reshape(f32[8,16,512]{2,1,0:T(8,128)} %param.7) | data formatting | bytes 524288 | tf_op jit(solution)/shard_map/reshape | solution.py:97
  93.3 7.6 %reduce_sum.37 = f32[4,8,256]{2,1,0:T(8,128)} reduce(f32[4,2,8,2,256,2]{5,4,3,2,1,0:T(8,128)} %reshape.21, f32[]{:T(128)} %constant.14.clone.1), dimensions={1,3,5}, to_apply=%region_1.2 | reduce | flops 57344 | bytes 294916 | tf_op jit(solution)/shard_map/reduce_sum | solution.py:98
  112.2 5.5 %collective-permute-start.18 = (f32[10,1,512]{2,1,0:T(1,128)S(1)}, f32[10,1,512]{2,1,0:T(1,128)S(1)}, u32[]{:S(2)}, u32[]{:S(2)}) collective-permute-start(f32[10,1,512]{2,1,0:T(1,128)S(1)} %get-tuple-element.23), channel_id=1, source_target_pairs={{1,0},{2,1},{3,2},{4,3},{5,4},{6,5},{7,6},{8,7},{9,8},{10,9},{11,1... | collective-permute-start | bytes 61448 | tf_op jit(solution)/shard_map/ppermute | solution.py:23
  119.6 3.6 %collective-permute-start.21 = (f32[1,8,256]{2,1,0:T(8,128)S(1)}, f32[1,8,256]{2,1,0:T(8,128)S(1)}, u32[]{:S(2)}, u32[]{:S(2)}) collective-permute-start(f32[1,8,256]{2,1,0:T(8,128)S(1)} %get-tuple-element.63), channel_id=1, source_target_pairs={{0,32},{32,64},{64,96},{96,128},{128,160},{160,192},{192,224},{1,3... | collective-permute-start | bytes 24584 | tf_op jit(solution)/shard_map/ppermute | solution.py:21
  123.2 18.1 %reshape.20 = f32[4,2,8,2,256,2]{5,4,3,2,1,0:T(8,128)} reshape(f32[8,16,512]{2,1,0:T(8,128)S(1)} %copy-done.1) | data formatting | bytes 524288 | tf_op jit(solution)/shard_map/reshape | solution.py:97
  141.3 7.0 %reduce_sum.36 = f32[4,8,256]{2,1,0:T(8,128)S(1)} reduce(f32[4,2,8,2,256,2]{5,4,3,2,1,0:T(8,128)} %reshape.20, f32[]{:T(128)} %constant.14.clone.1), dimensions={1,3,5}, to_apply=%region_0.1 | reduce | flops 57344 | bytes 294916 | tf_op jit(solution)/shard_map/reduce_sum | solution.py:98
  155.4 5.5 %collective-permute-start.22 = (f32[6,1,256]{2,1,0:T(1,128)S(1)}, f32[6,1,256]{2,1,0:T(1,128)S(1)}, u32[]{:S(2)}, u32[]{:S(2)}) collective-permute-start(f32[6,1,256]{2,1,0:T(1,128)S(1)} %get-tuple-element.53), channel_id=1, source_target_pairs={{1,0},{2,1},{3,2},{4,3},{5,4},{6,5},{7,6},{8,7},{9,8},{10,9},{11,1... | collective-permute-start | bytes 18440 | tf_op jit(solution)/shard_map/ppermute | solution.py:23
  162.9 5.7 %collective-permute-start.26 = (f32[10,1,512]{2,1,0:T(1,128)S(1)}, f32[10,1,512]{2,1,0:T(1,128)S(1)}, u32[]{:S(2)}, u32[]{:S(2)}) collective-permute-start(f32[10,1,512]{2,1,0:T(1,128)S(1)} %get-tuple-element.21), channel_id=1, source_target_pairs={{1,0},{2,1},{3,2},{4,3},{5,4},{6,5},{7,6},{8,7},{9,8},{10,9},{11,1... | collective-permute-start | bytes 61448 | tf_op jit(solution)/shard_map/ppermute | solution.py:23
  170.0 18.1 %reshape.22 = f32[4,2,8,2,256,2]{5,4,3,2,1,0:T(8,128)} reshape(f32[8,16,512]{2,1,0:T(8,128)S(1)} %fusion.4) | data formatting | bytes 524288 | tf_op jit(solution)/shard_map/reshape | solution.py:97
  188.0 7.0 %reduce_sum.38 = f32[4,8,256]{2,1,0:T(8,128)S(1)} reduce(f32[4,2,8,2,256,2]{5,4,3,2,1,0:T(8,128)} %reshape.22, f32[]{:T(128)} %constant.14.clone.1), dimensions={1,3,5}, to_apply=%region_2.3 | reduce | flops 57344 | bytes 294916 | tf_op jit(solution)/shard_map/reduce_sum | solution.py:98
  195.1 4.9 %collective-permute-start.29 = (f32[1,8,256]{2,1,0:T(8,128)S(1)}, f32[1,8,256]{2,1,0:T(8,128)S(1)}, u32[]{:S(2)}, u32[]{:S(2)}) collective-permute-start(f32[1,8,256]{2,1,0:T(8,128)S(1)} %get-tuple-element.60), channel_id=1, source_target_pairs={{0,32},{32,64},{64,96},{96,128},{128,160},{160,192},{192,224},{1,3... | collective-permute-start | bytes 24584 | tf_op jit(solution)/shard_map/ppermute | solution.py:21
  206.9 6.0 %collective-permute-start.30 = (f32[6,1,256]{2,1,0:T(1,128)S(1)}, f32[6,1,256]{2,1,0:T(1,128)S(1)}, u32[]{:S(2)}, u32[]{:S(2)}) collective-permute-start(f32[6,1,256]{2,1,0:T(1,128)S(1)} %get-tuple-element.51), channel_id=1, source_target_pairs={{1,0},{2,1},{3,2},{4,3},{5,4},{6,5},{7,6},{8,7},{9,8},{10,9},{11,1... | collective-permute-start | bytes 18440 | tf_op jit(solution)/shard_map/ppermute | solution.py:23
  223.7 6.0 %collective-permute-start.34 = (f32[6,1,256]{2,1,0:T(1,128)S(1)}, f32[6,1,256]{2,1,0:T(1,128)S(1)}, u32[]{:S(2)}, u32[]{:S(2)}) collective-permute-start(f32[6,1,256]{2,1,0:T(1,128)S(1)} %get-tuple-element.49), channel_id=1, source_target_pairs={{1,0},{2,1},{3,2},{4,3},{5,4},{6,5},{7,6},{8,7},{9,8},{10,9},{11,1... | collective-permute-start | bytes 18440 | tf_op jit(solution)/shard_map/ppermute | solution.py:23
  240.4 6.0 %collective-permute-start.38 = (f32[6,1,256]{2,1,0:T(1,128)S(1)}, f32[6,1,256]{2,1,0:T(1,128)S(1)}, u32[]{:S(2)}, u32[]{:S(2)}) collective-permute-start(f32[6,1,256]{2,1,0:T(1,128)S(1)} %get-tuple-element.47), channel_id=1, source_target_pairs={{1,0},{2,1},{3,2},{4,3},{5,4},{6,5},{7,6},{8,7},{9,8},{10,9},{11,1... | collective-permute-start | bytes 18440 | tf_op jit(solution)/shard_map/ppermute | solution.py:23
  257.2 6.0 %collective-permute-start.42 = (f32[6,1,256]{2,1,0:T(1,128)S(1)}, f32[6,1,256]{2,1,0:T(1,128)S(1)}, u32[]{:S(2)}, u32[]{:S(2)}) collective-permute-start(f32[6,1,256]{2,1,0:T(1,128)S(1)} %get-tuple-element.45), channel_id=1, source_target_pairs={{1,0},{2,1},{3,2},{4,3},{5,4},{6,5},{7,6},{8,7},{9,8},{10,9},{11,1... | collective-permute-start | bytes 18440 | tf_op jit(solution)/shard_map/ppermute | solution.py:23
  263.2 6.4 %broadcast_in_dim.2 = f32[4,2,8,2,256,2]{5,4,3,2,1,0:T(8,128)} broadcast(f32[4,8,256]{2,1,0:T(8,128)S(1)} %fusion.136), dimensions={0,2,4} | broadcast | bytes 294912 | tf_op jit(solution)/shard_map/broadcast_in_dim | solution.py:103
  269.6 12.7 %reshape.23 = f32[8,16,512]{2,1,0:T(8,128)S(1)} reshape(f32[4,2,8,2,256,2]{5,4,3,2,1,0:T(8,128)} %broadcast_in_dim.2) | data formatting | bytes 524288 | tf_op jit(solution)/shard_map/reshape | solution.py:104
  285.6 12.3 %all_gather.3 = f32[16,4,128]{2,1,0:T(4,128)S(1)} all-gather(f32[2,4,128]{2,1,0:T(4,128)S(1)} %broadcast_multiply_fusion.2), channel_id=1, replica_groups=mesh['gx'=8,'yz'=32] {'gx'}, dimensions={0}, use_global_device_ids=true | all-gather | bytes 36864 | tf_op jit(solution)/shard_map/all_gather | solution.py:121
  (142 shorter events, 107.9 us)
Async XLA Ops:
  1.4 13.0 %collective-permute-start.4 = (f32[1,16,512]{2,1,0:T(8,128)S(1)}, f32[1,16,512]{2,1,0:T(8,128)S(1)}, u32[]{:S(2)}, u32[]{:S(2)}) collective-permute-start(f32[1,16,512]{2,1,0:T(8,128)S(1)} %get-tuple-element.42), channel_id=1, source_target_pairs={{32,0},{64,32},{96,64},{128,96},{160,128},{192,160},{224,192},{33,... | collective-permute-start | bytes 98312 | tf_op jit(solution)/shard_map/ppermute | solution.py:23
  4.0 9.5 %collective-permute-start.5 = (f32[1,16,512]{2,1,0:T(8,128)S(1)}, f32[1,16,512]{2,1,0:T(8,128)S(1)}, u32[]{:S(2)}, u32[]{:S(2)}) collective-permute-start(f32[1,16,512]{2,1,0:T(8,128)S(1)} %get-tuple-element.43), channel_id=1, source_target_pairs={{0,32},{32,64},{64,96},{96,128},{128,160},{160,192},{192,224},{1,3... | collective-permute-start | bytes 98312 | tf_op jit(solution)/shard_map/ppermute | solution.py:21
  7.9 17.3 %collective-permute-start = (f32[1,16,512]{2,1,0:T(8,128)S(1)}, f32[1,16,512]{2,1,0:T(8,128)S(1)}, u32[]{:S(2)}, u32[]{:S(2)}) collective-permute-start(f32[1,16,512]{2,1,0:T(8,128)S(1)} %get-tuple-element.40), channel_id=1, source_target_pairs={{32,0},{64,32},{96,64},{128,96},{160,128},{192,160},{224,192},{33,... | collective-permute-start | bytes 98312 | tf_op jit(solution)/shard_map/ppermute | solution.py:23
  15.5 17.2 %collective-permute-start.7 = (f32[10,1,512]{2,1,0:T(1,128)S(1)}, f32[10,1,512]{2,1,0:T(1,128)S(1)}, u32[]{:S(2)}, u32[]{:S(2)}) collective-permute-start(f32[10,1,512]{2,1,0:T(1,128)S(1)} %get-tuple-element.30), channel_id=1, source_target_pairs={{0,1},{1,2},{2,3},{3,4},{4,5},{5,6},{6,7},{7,8},{8,9},{9,10},{10,1... | collective-permute-start | bytes 61448 | tf_op jit(solution)/shard_map/ppermute | solution.py:21
  19.1 13.6 %collective-permute-start.6 = (f32[10,1,512]{2,1,0:T(1,128)S(1)}, f32[10,1,512]{2,1,0:T(1,128)S(1)}, u32[]{:S(2)}, u32[]{:S(2)}) collective-permute-start(f32[10,1,512]{2,1,0:T(1,128)S(1)} %get-tuple-element.31), channel_id=1, source_target_pairs={{1,0},{2,1},{3,2},{4,3},{5,4},{6,5},{7,6},{8,7},{9,8},{10,9},{11,1... | collective-permute-start | bytes 61448 | tf_op jit(solution)/shard_map/ppermute | solution.py:23
  25.3 7.8 %collective-permute-start.3 = (f32[10,1,512]{2,1,0:T(1,128)S(1)}, f32[10,1,512]{2,1,0:T(1,128)S(1)}, u32[]{:S(2)}, u32[]{:S(2)}) collective-permute-start(f32[10,1,512]{2,1,0:T(1,128)S(1)} %get-tuple-element.28), channel_id=1, source_target_pairs={{0,1},{1,2},{2,3},{3,4},{4,5},{5,6},{6,7},{7,8},{8,9},{9,10},{10,1... | collective-permute-start | bytes 61448 | tf_op jit(solution)/shard_map/ppermute | solution.py:21
  36.2 7.5 %collective-permute-start.9 = (f32[1,16,512]{2,1,0:T(8,128)S(1)}, f32[1,16,512]{2,1,0:T(8,128)S(1)}, u32[]{:S(2)}, u32[]{:S(2)}) collective-permute-start(f32[1,16,512]{2,1,0:T(8,128)S(1)} %get-tuple-element.38), channel_id=1, source_target_pairs={{0,32},{32,64},{64,96},{96,128},{128,160},{160,192},{192,224},{1,3... | collective-permute-start | bytes 98312 | tf_op jit(solution)/shard_map/ppermute | solution.py:21
  47.1 8.0 %collective-permute-start.11 = (f32[10,1,512]{2,1,0:T(1,128)S(1)}, f32[10,1,512]{2,1,0:T(1,128)S(1)}, u32[]{:S(2)}, u32[]{:S(2)}) collective-permute-start(f32[10,1,512]{2,1,0:T(1,128)S(1)} %get-tuple-element.26), channel_id=1, source_target_pairs={{0,1},{1,2},{2,3},{3,4},{4,5},{5,6},{6,7},{7,8},{8,9},{9,10},{10,1... | collective-permute-start | bytes 61448 | tf_op jit(solution)/shard_map/ppermute | solution.py:21
  66.3 34.6 %collective-permute-start.15 = (f32[10,1,512]{2,1,0:T(1,128)S(1)}, f32[10,1,512]{2,1,0:T(1,128)S(1)}, u32[]{:S(2)}, u32[]{:S(2)}) collective-permute-start(f32[10,1,512]{2,1,0:T(1,128)S(1)} %get-tuple-element.24), channel_id=1, source_target_pairs={{0,1},{1,2},{2,3},{3,4},{4,5},{5,6},{6,7},{7,8},{8,9},{9,10},{10,1... | collective-permute-start | bytes 61448 | tf_op jit(solution)/shard_map/ppermute | solution.py:21
  69.2 31.7 %collective-permute-start.14 = (f32[10,1,512]{2,1,0:T(1,128)S(1)}, f32[10,1,512]{2,1,0:T(1,128)S(1)}, u32[]{:S(2)}, u32[]{:S(2)}) collective-permute-start(f32[10,1,512]{2,1,0:T(1,128)S(1)} %get-tuple-element.25), channel_id=1, source_target_pairs={{1,0},{2,1},{3,2},{4,3},{5,4},{6,5},{7,6},{8,7},{9,8},{10,9},{11,1... | collective-permute-start | bytes 61448 | tf_op jit(solution)/shard_map/ppermute | solution.py:23
  110.2 38.1 %collective-permute-start.19 = (f32[10,1,512]{2,1,0:T(1,128)S(1)}, f32[10,1,512]{2,1,0:T(1,128)S(1)}, u32[]{:S(2)}, u32[]{:S(2)}) collective-permute-start(f32[10,1,512]{2,1,0:T(1,128)S(1)} %get-tuple-element.22), channel_id=1, source_target_pairs={{0,1},{1,2},{2,3},{3,4},{4,5},{5,6},{6,7},{7,8},{8,9},{9,10},{10,1... | collective-permute-start | bytes 61448 | tf_op jit(solution)/shard_map/ppermute | solution.py:21
  112.2 36.1 %collective-permute-start.18 = (f32[10,1,512]{2,1,0:T(1,128)S(1)}, f32[10,1,512]{2,1,0:T(1,128)S(1)}, u32[]{:S(2)}, u32[]{:S(2)}) collective-permute-start(f32[10,1,512]{2,1,0:T(1,128)S(1)} %get-tuple-element.23), channel_id=1, source_target_pairs={{1,0},{2,1},{3,2},{4,3},{5,4},{6,5},{7,6},{8,7},{9,8},{10,9},{11,1... | collective-permute-start | bytes 61448 | tf_op jit(solution)/shard_map/ppermute | solution.py:23
  117.7 35.8 %collective-permute-start.20 = (f32[1,8,256]{2,1,0:T(8,128)S(1)}, f32[1,8,256]{2,1,0:T(8,128)S(1)}, u32[]{:S(2)}, u32[]{:S(2)}) collective-permute-start(f32[1,8,256]{2,1,0:T(8,128)S(1)} %get-tuple-element.62), channel_id=1, source_target_pairs={{32,0},{64,32},{96,64},{128,96},{160,128},{192,160},{224,192},{33,... | collective-permute-start | bytes 24584 | tf_op jit(solution)/shard_map/ppermute | solution.py:23
  119.6 33.9 %collective-permute-start.21 = (f32[1,8,256]{2,1,0:T(8,128)S(1)}, f32[1,8,256]{2,1,0:T(8,128)S(1)}, u32[]{:S(2)}, u32[]{:S(2)}) collective-permute-start(f32[1,8,256]{2,1,0:T(8,128)S(1)} %get-tuple-element.63), channel_id=1, source_target_pairs={{0,32},{32,64},{64,96},{96,128},{128,160},{160,192},{192,224},{1,3... | collective-permute-start | bytes 24584 | tf_op jit(solution)/shard_map/ppermute | solution.py:21
  149.1 11.8 %collective-permute-start.25 = (f32[1,16,512]{2,1,0:T(8,128)S(1)}, f32[1,16,512]{2,1,0:T(8,128)S(1)}, u32[]{:S(2)}, u32[]{:S(2)}) collective-permute-start(f32[1,16,512]{2,1,0:T(8,128)S(1)} %get-tuple-element.32), channel_id=1, source_target_pairs={{0,32},{32,64},{64,96},{96,128},{128,160},{160,192},{192,224},{1,3... | collective-permute-start | bytes 98312 | tf_op jit(solution)/shard_map/ppermute | solution.py:21
  151.0 9.9 %collective-permute-start.24 = (f32[1,16,512]{2,1,0:T(8,128)S(1)}, f32[1,16,512]{2,1,0:T(8,128)S(1)}, u32[]{:S(2)}, u32[]{:S(2)}) collective-permute-start(f32[1,16,512]{2,1,0:T(8,128)S(1)} %get-tuple-element.33), channel_id=1, source_target_pairs={{32,0},{64,32},{96,64},{128,96},{160,128},{192,160},{224,192},{33,... | collective-permute-start | bytes 98312 | tf_op jit(solution)/shard_map/ppermute | solution.py:23
  153.5 15.1 %collective-permute-start.23 = (f32[6,1,256]{2,1,0:T(1,128)S(1)}, f32[6,1,256]{2,1,0:T(1,128)S(1)}, u32[]{:S(2)}, u32[]{:S(2)}) collective-permute-start(f32[6,1,256]{2,1,0:T(1,128)S(1)} %get-tuple-element.52), channel_id=1, source_target_pairs={{0,1},{1,2},{2,3},{3,4},{4,5},{5,6},{6,7},{7,8},{8,9},{9,10},{10,1... | collective-permute-start | bytes 18440 | tf_op jit(solution)/shard_map/ppermute | solution.py:21
  155.4 13.1 %collective-permute-start.22 = (f32[6,1,256]{2,1,0:T(1,128)S(1)}, f32[6,1,256]{2,1,0:T(1,128)S(1)}, u32[]{:S(2)}, u32[]{:S(2)}) collective-permute-start(f32[6,1,256]{2,1,0:T(1,128)S(1)} %get-tuple-element.53), channel_id=1, source_target_pairs={{1,0},{2,1},{3,2},{4,3},{5,4},{6,5},{7,6},{8,7},{9,8},{10,9},{11,1... | collective-permute-start | bytes 18440 | tf_op jit(solution)/shard_map/ppermute | solution.py:23
  161.0 7.8 %collective-permute-start.27 = (f32[10,1,512]{2,1,0:T(1,128)S(1)}, f32[10,1,512]{2,1,0:T(1,128)S(1)}, u32[]{:S(2)}, u32[]{:S(2)}) collective-permute-start(f32[10,1,512]{2,1,0:T(1,128)S(1)} %get-tuple-element.20), channel_id=1, source_target_pairs={{0,1},{1,2},{2,3},{3,4},{4,5},{5,6},{6,7},{7,8},{8,9},{9,10},{10,1... | collective-permute-start | bytes 61448 | tf_op jit(solution)/shard_map/ppermute | solution.py:21
  205.0 8.0 %collective-permute-start.31 = (f32[6,1,256]{2,1,0:T(1,128)S(1)}, f32[6,1,256]{2,1,0:T(1,128)S(1)}, u32[]{:S(2)}, u32[]{:S(2)}) collective-permute-start(f32[6,1,256]{2,1,0:T(1,128)S(1)} %get-tuple-element.50), channel_id=1, source_target_pairs={{0,1},{1,2},{2,3},{3,4},{4,5},{5,6},{6,7},{7,8},{8,9},{9,10},{10,1... | collective-permute-start | bytes 18440 | tf_op jit(solution)/shard_map/ppermute | solution.py:21
  221.8 8.0 %collective-permute-start.35 = (f32[6,1,256]{2,1,0:T(1,128)S(1)}, f32[6,1,256]{2,1,0:T(1,128)S(1)}, u32[]{:S(2)}, u32[]{:S(2)}) collective-permute-start(f32[6,1,256]{2,1,0:T(1,128)S(1)} %get-tuple-element.48), channel_id=1, source_target_pairs={{0,1},{1,2},{2,3},{3,4},{4,5},{5,6},{6,7},{7,8},{8,9},{9,10},{10,1... | collective-permute-start | bytes 18440 | tf_op jit(solution)/shard_map/ppermute | solution.py:21
  238.5 8.0 %collective-permute-start.39 = (f32[6,1,256]{2,1,0:T(1,128)S(1)}, f32[6,1,256]{2,1,0:T(1,128)S(1)}, u32[]{:S(2)}, u32[]{:S(2)}) collective-permute-start(f32[6,1,256]{2,1,0:T(1,128)S(1)} %get-tuple-element.46), channel_id=1, source_target_pairs={{0,1},{1,2},{2,3},{3,4},{4,5},{5,6},{6,7},{7,8},{8,9},{9,10},{10,1... | collective-permute-start | bytes 18440 | tf_op jit(solution)/shard_map/ppermute | solution.py:21
  255.3 27.8 %collective-permute-start.43 = (f32[6,1,256]{2,1,0:T(1,128)S(1)}, f32[6,1,256]{2,1,0:T(1,128)S(1)}, u32[]{:S(2)}, u32[]{:S(2)}) collective-permute-start(f32[6,1,256]{2,1,0:T(1,128)S(1)} %get-tuple-element.44), channel_id=1, source_target_pairs={{0,1},{1,2},{2,3},{3,4},{4,5},{5,6},{6,7},{7,8},{8,9},{9,10},{10,1... | collective-permute-start | bytes 18440 | tf_op jit(solution)/shard_map/ppermute | solution.py:21
  257.2 25.9 %collective-permute-start.42 = (f32[6,1,256]{2,1,0:T(1,128)S(1)}, f32[6,1,256]{2,1,0:T(1,128)S(1)}, u32[]{:S(2)}, u32[]{:S(2)}) collective-permute-start(f32[6,1,256]{2,1,0:T(1,128)S(1)} %get-tuple-element.45), channel_id=1, source_target_pairs={{1,0},{2,1},{3,2},{4,3},{5,4},{6,5},{7,6},{8,7},{9,8},{10,9},{11,1... | collective-permute-start | bytes 18440 | tf_op jit(solution)/shard_map/ppermute | solution.py:23
  (27 other events, 266.6 us)
where the time goes:
time: 301 us; the launch traced here: 299 us
  starting transfers between devices  146 us (49%)
  local copies, waits for them, and re-layouts  80.7 us (27%)
  other arithmetic  33 us (11%)
  waiting for transfers between devices  25.3 us (8%)
  blocking collectives  12.3 us (4%)
    ppermute x22, starting transfers between devices, padded_2(): lax.ppermute(head, axis, [((i + 1) % count, i) for i in range(ends)])  86 us
    ppermute x22, starting transfers between devices, padded_2(): lax.ppermute(tail, axis, [(i, (i + 1) % count) for i in range(ends)])  59.7 us
    reshape x4, local copies, waits for them, and re-layouts, restrict(): blocks = field.reshape(size_a // 2, 2, size_b // 2, 2, size_c // 2, 2)  57 us
    ppermute x22, waiting for transfers between devices, padded_2(): lax.ppermute(head, axis, [((i + 1) % count, i) for i in range(ends)])  25.2 us
    reduce_sum x4, other arithmetic, restrict(): return jnp.sum(blocks, axis=(1, 3, 5)) * 0.125  21.8 us
    reshape x1, local copies, waits for them, and re-layouts, prolong(): return wide.reshape(2 * size_a, 2 * size_b, 2 * size_c)  12.7 us
    all_gather x1, blocking collectives, on_device(): coarsest = lax.all_gather(restrict(coarse_resid), 'gx', axis=0, tiled=True)  12.3 us
    broadcast_in_dim x1, local copies, waits for them, and re-layouts, prolong(): jnp.broadcast_to(field[:, None, :, None, :, None], (size_a, 2, size_b, 2,...  6.38 us
  transfers between devices with their start and end apart: 44, of which 13 were waited for; matrix products, arithmetic and copies ran while one was open for 26% of the time, Pallas kernels for 0%

commit v1 on v0

v1 whole, which is shorter than its diff:
```python
import functools

import jax
import jax.numpy as jnp
from jax import lax
from jax.experimental import pallas as pl
from jax.experimental.pallas import tpu as pltpu
from jax.sharding import PartitionSpec as P

DEGREE = 4
THETA = 1.125
DELTA = 0.875
MESH = pl.DeviceIdType.MESH
F32 = jnp.float32

NX, NY, NZ = 8, 16, 512
CX, CY, CZ = 4, 8, 256
ROUNDS = DEGREE + 1


def cheb_terms():
    sigma = THETA / DELTA
    rho_prev = 1.0 / sigma
    terms = []
    for _ in range(DEGREE - 1):
        rho_next = 1.0 / (2.0 * sigma - rho_prev)
        terms.append((rho_next * rho_prev, 2.0 * rho_next / DELTA))
        rho_prev = rho_next
    return terms


def lanes(shape):
    return lax.broadcasted_iota(jnp.int32, shape, 1)


def rows(shape):
    return lax.broadcasted_iota(jnp.int32, shape, 0)


def halve_z(field):
    count, width = field.shape
    lane = lanes((count, 128))
    even = jnp.where(lane < 64, 2 * lane, 2 * lane - 128)
    low = lane < 64
    tiles = []
    for t in range(width // 256):
        halves = []
        for h in range(2):
            part = field[:, (2 * t + h) * 128 : (2 * t + h + 1) * 128]
            part = part + pltpu.roll(part, 127, 1)
            halves.append(jnp.take_along_axis(part, even, axis=1))
        tiles.append(jnp.where(low, halves[0], halves[1]))
    return tiles[0] if len(tiles) == 1 else jnp.concatenate(tiles, axis=1)


def double_z(field):
    count, width = field.shape
    half = lanes((count, 128)) // 2
    tiles = []
    for t in range(width // 128):
        part = field[:, t * 128 : (t + 1) * 128]
        tiles.append(jnp.take_along_axis(part, half, axis=1))
        tiles.append(jnp.take_along_axis(part, half + 64, axis=1))
    return jnp.concatenate(tiles, axis=1)


def z_beside(field):
    width = field.shape[1]
    return pltpu.roll(field, width - 1, 1), pltpu.roll(field, 1, 1)


def y_beside(field, below, above):
    count = field.shape[0]
    row = rows(field.shape)
    up = jnp.where(row == count - 1, jnp.broadcast_to(above, field.shape), pltpu.roll(field, count - 1, 0))
    down = jnp.where(row == 0, jnp.broadcast_to(below, field.shape), pltpu.roll(field, 1, 0))
    return up, down


def kernel(
    guess_h, rhs_h, alpha_h, beta_h, out_ref, last_ref,
    gb, rhs, alpha, xs, ds, gs, diag, ws, hx, hy, sy, hx0, hy0, sy0,
    pair, wide, cab, cg, cw, cxs, cds, cdiag, coarsest,
    load_sem, sx_sem, rx_sem, sy_sem, ry_sem, sab_sem, rab_sem, sg_sem, rg_sem, sl_sem, rl_sem,
):
    gx = lax.axis_index("gx")
    yz = lax.axis_index("yz")
    ngx = lax.axis_size("gx")
    nyz = lax.axis_size("yz")

    def at(dx, dy):
        return (lax.rem(gx + ngx + dx, ngx), lax.rem(yz + nyz + dy, nyz))

    loads = []
    for k, (src, dst) in enumerate(
        ((guess_h, gb.at[0]), (beta_h, gb.at[1]), (alpha_h, alpha), (rhs_h, rhs))
    ):
        copy = pltpu.make_async_copy(src, dst, load_sem.at[k])
        copy.start()
        loads.append(copy)

    around = [(dx, dy) for dx in (-1, 0, 1) for dy in (-1, 0, 1) if (dx, dy) != (0, 0)]
    peers = [(dx, 0) for dx in range(1, 8)]
    greet = [at(dx, dy) for dx, dy in peers] + [at(dx, dy) for dx, dy in around if dy != 0]
    barrier = pltpu.get_barrier_semaphore()
    for device in greet:
        pl.semaphore_signal(barrier, inc=1, device_id=device, device_id_type=MESH)
    loads[0].wait()
    loads[1].wait()
    for f in range(2):
        for p in range(NX):
            sy0[0, f, p : p + 1, :] = gb[f, p, NY - 1 : NY, :]
            sy0[1, f, p : p + 1, :] = gb[f, p, 0:1, :]
    pl.semaphore_wait(barrier, len(greet))

    sent, done = [], []

    def send(src, dst, s_sem, r_sem, device):
        copy = pltpu.make_async_remote_copy(
            src_ref=src, dst_ref=dst, send_sem=s_sem, recv_sem=r_sem, device_id=device, device_id_type=MESH
        )
        copy.start()
        sent.append(copy)
        return copy

    waits = [
        send(sy0.at[0], hy0.at[0], sy_sem.at[0, 0], ry_sem.at[0, 0], at(0, 1)),
        send(sy0.at[1], hy0.at[1], sy_sem.at[0, 1], ry_sem.at[0, 1], at(0, -1)),
        send(gb.at[:, NX - 1], hx0.at[0], sx_sem.at[0, 0], rx_sem.at[0, 0], at(1, 0)),
        send(gb.at[:, 0], hx0.at[1], sx_sem.at[0, 1], rx_sem.at[0, 1], at(-1, 0)),
    ]

    loads[2].wait()
    loads[3].wait()

    def restrict_pair(first, second):
        both = first + second
        for t in range(4):
            pair[t] = both[:, t * 128 : (t + 1) * 128]
        summed = jnp.concatenate(
            [pair[t, pl.ds(0, CY, 2), :] + pair[t, pl.ds(1, CY, 2), :] for t in range(4)], axis=1
        )
        return halve_z(summed)

    for q in range(CX):
        cab[1, 1, 0, q] = 0.125 * restrict_pair(alpha[2 * q], alpha[2 * q + 1])
        cab[1, 1, 1, q] = 0.125 * restrict_pair(gb[1, 2 * q], gb[1, 2 * q + 1])
    ab_waits = [
        send(cab.at[1, 1], cab.at[1 - dx, 1 - dy], sab_sem.at[k], rab_sem.at[k], at(dx, dy))
        for k, (dx, dy) in enumerate(around)
    ]

    in_lo_x = (gx > 0).astype(F32)
    in_hi_x = (gx < ngx - 1).astype(F32)
    in_lo_y = (yz > 0).astype(F32)
    in_hi_y = (yz < nyz - 1).astype(F32)

    for copy in waits:
        copy.wait_recv()

    terms = [(None, 1.0 / THETA)] + cheb_terms()

    def spread(x_at, below, above, w):
        x = x_at(0)
        up, down = y_beside(x, below, above)
        right, left = z_beside(x)
        return (
            w(0) * x_at(1) + w(1) * x_at(-1) + w(2) * up + w(3) * down + w(4) * right + w(5) * left
        )

    lane = lanes((NY, NZ))
    row = rows((NY, NZ))
    for p in range(NX):
        b = gb[1, p]
        b_hi = gb[1, p + 1] if p < NX - 1 else hx0[1, 1] * in_hi_x
        b_lo = gb[1, p - 1] if p > 0 else hx0[0, 1] * in_lo_x
        b_up, b_down = y_beside(
            b, hy0[0, 1, p : p + 1, :] * in_lo_y, hy0[1, 1, p : p + 1, :] * in_hi_y
        )
        b_right, b_left = z_beside(b)
        b_right = jnp.where(lane == NZ - 1, 0.0, b_right)
        b_left = jnp.where(lane == 0, 0.0, b_left)
        faces = [0.5 * (b + other) for other in (b_hi, b_lo, b_up, b_down, b_right, b_left)]
        total = faces[0] + faces[1] + faces[2] + faces[3] + faces[4] + faces[5]
        whole = alpha[p] + total
        diag[p] = whole
        inverse = 1.0 / whole
        w = [inverse * face for face in faces]
        if p == NX - 1:
            w[0] = w[0] * in_hi_x
        if p == 0:
            w[1] = w[1] * in_lo_x
        w[2] = jnp.where(row == NY - 1, w[2] * in_hi_y, w[2])
        w[3] = jnp.where(row == 0, w[3] * in_lo_y, w[3])
        w[4] = jnp.where(lane == NZ - 1, 0.0, w[4])
        w[5] = jnp.where(lane == 0, 0.0, w[5])
        for e in range(6):
            ws[e, p] = w[e]
        g = inverse * rhs[p]
        gs[p] = g

        def x_at(step, p=p):
            if p + step < 0:
                return hx0[0, 0]
            if p + step >= NX:
                return hx0[1, 0]
            return gb[0, p + step]

        x = gb[0, p]
        resid = g - x + spread(x_at, hy0[0, 0, p : p + 1, :], hy0[1, 0, p : p + 1, :], lambda e: w[e])
        update = resid * (1.0 / THETA)
        ds[p] = update
        xs[0, p] = x + update

    def post(r, cur):
        for p in range(NX):
            sy[r, 0, p : p + 1, :] = xs[cur, p, NY - 1 : NY, :]
            sy[r, 1, p : p + 1, :] = xs[cur, p, 0:1, :]
        return [
            send(sy.at[r, 0], hy.at[r, 0], sy_sem.at[r + 1, 0], ry_sem.at[r + 1, 0], at(0, 1)),
            send(sy.at[r, 1], hy.at[r, 1], sy_sem.at[r + 1, 1], ry_sem.at[r + 1, 1], at(0, -1)),
            send(xs.at[cur, NX - 1], hx.at[r, 0], sx_sem.at[r + 1, 0], rx_sem.at[r + 1, 0], at(1, 0)),
            send(xs.at[cur, 0], hx.at[r, 1], sx_sem.at[r + 1, 1], rx_sem.at[r + 1, 1], at(-1, 0)),
        ]

    def residual(r, cur, p):
        def x_at(step):
            if p + step < 0:
                return hx[r, 0]
            if p + step >= NX:
                return hx[r, 1]
            return xs[cur, p + step]

        return (
            gs[p]
            - xs[cur, p]
            + spread(x_at, hy[r, 0, p : p + 1, :], hy[r, 1, p : p + 1, :], lambda e: ws[e, p])
        )

    slot_in_x = (in_lo_x, None, in_hi_x)
    slot_in_y = (in_lo_y, None, in_hi_y)

    def slot_mask(i, j):
        masks = [m for m in (slot_in_x[i], slot_in_y[j]) if m is not None]
        if not masks:
            return None
        return masks[0] if len(masks) == 1 else masks[0] * masks[1]

    def masked(value, i, j):
        mask = slot_mask(i, j)
        return value if mask is None else value * mask

    def coarse_y(get, i, q, j):
        here = get(i, j, q)
        below = get(i, j - 1, q)[CY - 1 : CY, :] if j > 0 else here[0:1, :]
        above = get(i, j + 1, q)[0:1, :] if j < 2 else here[CY - 1 : CY, :]
        return y_beside(here, below, above)

    def coarse_slots(depth):
        found = []
        for plane in range(-depth, CX + depth):
            beyond = max(-plane, plane - CX + 1, 0)
            i, q = (plane + CX) // CX, (plane + CX) % CX
            for j in (0, 1, 2) if beyond < depth else (1,):
                found.append((plane, i, q, j))
        return found

    def coarse_setup():
        clane = lanes((CY, CZ))

        def beta(i, j, q):
            return masked(cab[i, j, 1, q], i, j)

        for plane, i, q, j in coarse_slots(3):
            b = beta(i, j, q)
            hi, lo = plane + 1 + CX, plane - 1 + CX
            b_hi = beta(hi // CX, j, hi % CX)
            b_lo = beta(lo // CX, j, lo % CX)
            b_up, b_down = coarse_y(beta, i, q, j)
            b_right, b_left = z_beside(b)
            b_right = jnp.where(clane == CZ - 1, 0.0, b_right)
            b_left = jnp.where(clane == 0, 0.0, b_left)
            faces = [0.5 * (b + other) for other in (b_hi, b_lo, b_up, b_down, b_right, b_left)]
            total = faces[0] + faces[1] + faces[2] + faces[3] + faces[4] + faces[5]
            whole = cab[i, j, 0, q] + 0.25 * total
            if (i, j) == (1, 1):
                cdiag[q] = whole
            scale = masked(0.25 / whole, i, j)
            w = [scale * face for face in faces]
            w[4] = jnp.where(clane == CZ - 1, 0.0, w[4])
            w[5] = jnp.where(clane == 0, 0.0, w[5])
            for e in range(6):
                cw[e, i, j, q] = w[e]

    cur = 0
    for r in range(ROUNDS - 1):
        round_waits = post(r, cur)
        if r == 1:
            for copy in ab_waits:
                copy.wait_recv()
            coarse_setup()
        for copy in round_waits:
            copy.wait_recv()
        if r > 0:
            for copy in earlier:
                copy.wait_send()
                done.append(id(copy))
        earlier = round_waits[2:]
        if r < ROUNDS - 2:
            first, second = terms[r + 1]
            for p in range(NX):
                update = first * ds[p] + second * residual(r, cur, p)
                ds[p] = update
                xs[1 - cur, p] = xs[cur, p] + update
            cur = 1 - cur
        else:
            for q in range(CX):
                a = diag[2 * q] * residual(r, cur, 2 * q)
                b = diag[2 * q + 1] * residual(r, cur, 2 * q + 1)
                cg[1, 1, q] = 0.125 * restrict_pair(a, b) / cdiag[q]

    g_waits = [
        send(cg.at[1, 1], cg.at[1 - dx, 1 - dy], sg_sem.at[k], rg_sem.at[k], at(dx, dy))
        for k, (dx, dy) in enumerate(around)
    ]
    for copy in g_waits:
        copy.wait_recv()

    def coarse_g(i, j, q):
        return masked(cg[i, j, q], i, j)

    for plane, i, q, j in coarse_slots(4):
        update = coarse_g(i, j, q) * (1.0 / THETA)
        cxs[0, i, j, q] = update
        cds[i, j, q] = update

    def coarse_residual(now, plane, i, q, j):
        def get(i, j, q):
            return cxs[now, i, j, q]

        x = get(i, j, q)
        hi, lo = plane + 1 + CX, plane - 1 + CX
        up, down = coarse_y(get, i, q, j)
        right, left = z_beside(x)
        return (
            coarse_g(i, j, q) - x
            + cw[0, i, j, q] * get(hi // CX, j, hi % CX)
            + cw[1, i, j, q] * get(lo // CX, j, lo % CX)
            + cw[2, i, j, q] * up
            + cw[3, i, j, q] * down
            + cw[4, i, j, q] * right
            + cw[5, i, j, q] * left
        )

    now = 0
    for step, (first, second) in enumerate(cheb_terms()):
        for plane, i, q, j in coarse_slots(3 - step):
            update = first * cds[i, j, q] + second * coarse_residual(now, plane, i, q, j)
            cds[i, j, q] = update
            cxs[1 - now, i, j, q] = cxs[now, i, j, q] + update
        now = 1 - now

    quarter = []
    for q in range(CX):
        quarter.append(cdiag[q] * coarse_residual(now, q, 1, q, 1))
    for h in range(CX // 2):
        both = quarter[2 * h] + quarter[2 * h + 1]
        for t in range(2):
            pair[t, 0:CY, :] = both[:, t * 128 : (t + 1) * 128]
        summed = jnp.concatenate(
            [pair[t, pl.ds(0, CY // 2, 2), :] + pair[t, pl.ds(1, CY // 2, 2), :] for t in range(2)], axis=1
        )
        coarsest[0, h] = 0.125 * halve_z(summed)
    l_waits = [
        send(coarsest.at[0], coarsest.at[dx], sl_sem.at[dx], rl_sem.at[dx], at(dx, 0)) for dx in range(1, 8)
    ]

    for q in range(CX):
        fine = double_z(cxs[now, 1, 1, q])
        for t in range(4):
            part = fine[:, t * 128 : (t + 1) * 128]
            wide[t, pl.ds(0, CY, 2), :] = part
            wide[t, pl.ds(1, CY, 2), :] = part
        full = jnp.concatenate([wide[t] for t in range(4)], axis=1)
        for p in (2 * q, 2 * q + 1):
            out_ref[p] = xs[cur, p] + full

    for copy in l_waits:
        copy.wait_recv()
    for dx in range(8):
        owner = lax.rem(gx + ngx - dx, ngx)
        last_ref[pl.ds(2 * owner, 2)] = coarsest[dx]
    for copy in sent:
        if id(copy) not in done:
            copy.wait_send()


def on_device(guess, rhs, alpha, beta):
    vmem = pltpu.VMEM
    dma = pltpu.SemaphoreType.DMA
    fine = (NX, NY, NZ)
    scratch = [
        vmem((2, *fine), F32), vmem(fine, F32), vmem(fine, F32), vmem((2, *fine), F32), vmem(fine, F32),
        vmem(fine, F32), vmem(fine, F32), vmem((6, *fine), F32),
        vmem((ROUNDS - 1, 2, NY, NZ), F32), vmem((ROUNDS - 1, 2, NX, NZ), F32), vmem((ROUNDS - 1, 2, NX, NZ), F32),
        vmem((2, 2, NY, NZ), F32), vmem((2, 2, NX, NZ), F32), vmem((2, 2, NX, NZ), F32),
        vmem((4, NY, 128), F32), vmem((4, NY, 128), F32),
        vmem((3, 3, 2, CX, CY, CZ), F32), vmem((3, 3, CX, CY, CZ), F32), vmem((6, 3, 3, CX, CY, CZ), F32),
        vmem((2, 3, 3, CX, CY, CZ), F32), vmem((3, 3, CX, CY, CZ), F32), vmem((CX, CY, CZ), F32),
        vmem((8, 2, CY // 2, CZ // 2), F32),
        dma((4,)), dma((ROUNDS, 2)), dma((ROUNDS, 2)), dma((ROUNDS, 2)), dma((ROUNDS, 2)),
        dma((8,)), dma((8,)), dma((8,)), dma((8,)), dma((8,)), dma((8,)),
    ]
    return pl.pallas_call(
        kernel,
        out_shape=(
            jax.ShapeDtypeStruct(fine, F32),
            jax.ShapeDtypeStruct((16, CY // 2, CZ // 2), F32),
        ),
        in_specs=[pl.BlockSpec(memory_space=pltpu.HBM)] * 4,
        out_specs=(pl.BlockSpec(memory_space=vmem), pl.BlockSpec(memory_space=vmem)),
        scratch_shapes=scratch,
        compiler_params=pltpu.CompilerParams(
            collective_id=0, has_side_effects=True, vmem_limit_bytes=60 << 20
        ),
        name="vcycle",
    )(guess, rhs, alpha, beta)


def solution(mesh):
    placed = (P("gx", "yz", None),) * 4
    return jax.shard_map(
        on_device,
        mesh=mesh,
        in_specs=placed,
        out_specs=(P("gx", "yz", None), P(None, "yz", None)),
        check_vma=False,
    )
```

time: 301 us -> 48.9 us (0.16)
  the two profiles are of different devices: /device:TPU:7 before, /device:TPU:1 now
where the time goes in v1:
time: 48.9 us; the launch traced here: 48.8 us
  Pallas kernels  45.9 us (94%)
  local copies, waits for them, and re-layouts  2.3 us (5%)
  between operations  0.65 us (1%)
    pallas_call x1, Pallas kernels, on_device(): pl.pallas_call(kernel, out_shape=(jax.ShapeDtypeStruct(fine, F32), jax.Sh...  45.9 us
    unnamed x4, local copies, waits for them, and re-layouts  2.3 us

profile of v1, /device:TPU:1, one launch (start us, length us, event | category | flops | bytes accessed | tf_op | source)
XLA Modules:
  0.0 48.8 jit_solution(13938816060935343675)
XLA Ops:
  0.6 45.9 %vcycle.1 = (f32[8,16,512]{2,1,0:T(8,128)}, f32[16,4,128]{2,1,0:T(4,128)}) custom-call(f32[8,16,512]{2,1,0:T(8,128)} %guess_h.1, f32[8,16,512]{2,1,0:T(8,128)} %rhs_h.1, f32[8,16,512]{2,1,0:T(8,128)} %alpha_h.1, f32[8,16,512]{2,1,0:T(8,128)} %beta_h.1), custom_call_target="tpu_custom_call" | custom-call | tf_op jit(solution)/shard_map/vcycle/pallas_call | solution.py:414
  46.5 0.0 copy-start
  46.5 1.7 %copy.8 = f32[8,16,512]{2,1,0:T(8,128)} copy(f32[8,16,512]{2,1,0:T(8,128)} %get-tuple-element.4) | data formatting | bytes 524288
  48.2 0.0 copy-done
  48.2 0.6 %copy.9 = f32[16,4,128]{2,1,0:T(4,128)} copy(f32[16,4,128]{2,1,0:T(4,128)S(1)} %copy-done) | data formatting | bytes 65536
Async XLA Ops:
  46.5 1.7 %copy-start = (f32[16,4,128]{2,1,0:T(4,128)S(1)}, f32[16,4,128]{2,1,0:T(4,128)}, u32[]{:S(2)}) copy-start(f32[16,4,128]{2,1,0:T(4,128)} %get-tuple-element.5) | copy-start | bytes 98308

commit v2 on v1

--- a/solution.py
+++ b/solution.py
@@ -15,7 +15,9 @@
 
 NX, NY, NZ = 8, 16, 512
 CX, CY, CZ = 4, 8, 256
-ROUNDS = DEGREE + 1
+DEPTH = DEGREE + 1
+PX, PY = DEPTH, 8
+EX, EY = NX + 2 * DEPTH, NY + 2 * PY
 
 
 def cheb_terms():
@@ -77,11 +79,19 @@
     return up, down
 
 
+def tile_a(p):
+    return 2 * p + (1 if p >= 4 else 0)
+
+
+def tile_b(p):
+    return 2 * p + (0 if p >= 4 else 1)
+
+
 def kernel(
     guess_h, rhs_h, alpha_h, beta_h, out_ref, last_ref,
-    gb, rhs, alpha, xs, ds, gs, diag, ws, hx, hy, sy, hx0, hy0, sy0,
+    xa, xb, be, al, rh, ds, gs, diag, ws, pk, rk, rc,
     pair, wide, cab, cg, cw, cxs, cds, cdiag, coarsest,
-    load_sem, sx_sem, rx_sem, sy_sem, ry_sem, sab_sem, rab_sem, sg_sem, rg_sem, sl_sem, rl_sem,
+    load_sem, sx_sem, rx_sem, sy_sem, ry_sem, sc_sem, rc_sem, sab_sem, rab_sem, sg_sem, rg_sem, sl_sem, rl_sem,
 ):
     gx = lax.axis_index("gx")
     yz = lax.axis_index("yz")
@@ -90,14 +100,6 @@
 
     def at(dx, dy):
         return (lax.rem(gx + ngx + dx, ngx), lax.rem(yz + nyz + dy, nyz))
-
-    loads = []
-    for k, (src, dst) in enumerate(
-        ((guess_h, gb.at[0]), (beta_h, gb.at[1]), (alpha_h, alpha), (rhs_h, rhs))
-    ):
-        copy = pltpu.make_async_copy(src, dst, load_sem.at[k])
-        copy.start()
-        loads.append(copy)
 
     around = [(dx, dy) for dx in (-1, 0, 1) for dy in (-1, 0, 1) if (dx, dy) != (0, 0)]
     peers = [(dx, 0) for dx in range(1, 8)]
@@ -105,15 +107,32 @@
     barrier = pltpu.get_barrier_semaphore()
     for device in greet:
         pl.semaphore_signal(barrier, inc=1, device_id=device, device_id_type=MESH)
-    loads[0].wait()
-    loads[1].wait()
-    for f in range(2):
+
+    own_x, own_y = pl.ds(PX, NX), pl.ds(PY, NY)
+    loads = []
+    for k, (src, dst) in enumerate(((guess_h, xa), (beta_h, be), (alpha_h, al), (rhs_h, rh))):
+        copy = pltpu.make_async_copy(src, dst.at[own_x, own_y], load_sem.at[k])
+        copy.start()
+        loads.append(copy)
+    for copy in loads:
+        copy.wait()
+
+    half = rows((8, NZ)) < 4
+
+    def packed(first, second, side):
+        moved = pltpu.roll(second, 4, 0)
+        return jnp.where(half, moved, first) if side == 0 else jnp.where(half, first, moved)
+
+    for side, start, fifth in ((0, PY + 8, PY + 11), (1, PY, PY + 4)):
+        tile = pl.ds(start, 8)
         for p in range(NX):
-            sy0[0, f, p : p + 1, :] = gb[f, p, NY - 1 : NY, :]
-            sy0[1, f, p : p + 1, :] = gb[f, p, 0:1, :]
+            pk[side, tile_a(p)] = packed(xa[PX + p, tile, :], be[PX + p, tile, :], side)
+            pk[side, tile_b(p)] = packed(al[PX + p, tile, :], rh[PX + p, tile, :], side)
+            pk[side, 16, p : p + 1, :] = xa[PX + p, fifth : fifth + 1, :]
+            pk[side, 17, p : p + 1, :] = be[PX + p, fifth : fifth + 1, :]
     pl.semaphore_wait(barrier, len(greet))
 
-    sent, done = [], []
+    sent = []
 
     def send(src, dst, s_sem, r_sem, device):
         copy = pltpu.make_async_remote_copy(
@@ -123,15 +142,35 @@
         sent.append(copy)
         return copy
 
-    waits = [
-        send(sy0.at[0], hy0.at[0], sy_sem.at[0, 0], ry_sem.at[0, 0], at(0, 1)),
-        send(sy0.at[1], hy0.at[1], sy_sem.at[0, 1], ry_sem.at[0, 1], at(0, -1)),
-        send(gb.at[:, NX - 1], hx0.at[0], sx_sem.at[0, 0], rx_sem.at[0, 0], at(1, 0)),
-        send(gb.at[:, 0], hx0.at[1], sx_sem.at[0, 1], rx_sem.at[0, 1], at(-1, 0)),
+    y_waits = [
+        send(pk.at[side], rk.at[side], sy_sem.at[side], ry_sem.at[side], at(0, 1 - 2 * side)) for side in (0, 1)
     ]
-
-    loads[2].wait()
-    loads[3].wait()
+    c_waits = []
+    for sx in (0, 1):
+        for sy in (0, 1):
+            part = pl.ds(9, 7) if sx == 0 else pl.ds(0, 7)
+            c_waits.append(
+                send(
+                    pk.at[sy, part], rc.at[sx, sy], sc_sem.at[sx, sy], rc_sem.at[sx, sy],
+                    at(1 - 2 * sx, 1 - 2 * sy),
+                )
+            )
+    x_waits = []
+    for k, (src, dst, deep) in enumerate(
+        ((guess_h, xa, DEPTH), (beta_h, be, DEPTH), (alpha_h, al, DEPTH - 1), (rhs_h, rh, DEPTH - 1))
+    ):
+        x_waits.append(
+            send(
+                src.at[pl.ds(NX - deep, deep)], dst.at[pl.ds(PX - deep, deep), own_y],
+                sx_sem.at[k, 0], rx_sem.at[k, 0], at(1, 0),
+            )
+        )
+        x_waits.append(
+            send(
+                src.at[pl.ds(0, deep)], dst.at[pl.ds(PX + NX, deep), own_y],
+                sx_sem.at[k, 1], rx_sem.at[k, 1], at(-1, 0),
+            )
+        )
 
     def restrict_pair(first, second):
         both = first + second
@@ -143,8 +182,9 @@
         return halve_z(summed)
 
     for q in range(CX):
-        cab[1, 1, 0, q] = 0.125 * restrict_pair(alpha[2 * q], alpha[2 * q + 1])
-        cab[1, 1, 1, q] = 0.125 * restrict_pair(gb[1, 2 * q], gb[1, 2 * q + 1])
+        one, two = PX + 2 * q, PX + 2 * q + 1
+        cab[1, 1, 0, q] = 0.125 * restrict_pair(al[one, own_y, :], al[two, own_y, :])
+        cab[1, 1, 1, q] = 0.125 * restrict_pair(be[one, own_y, :], be[two, own_y, :])
     ab_waits = [
         send(cab.at[1, 1], cab.at[1 - dx, 1 - dy], sab_sem.at[k], rab_sem.at[k], at(dx, dy))
         for k, (dx, dy) in enumerate(around)
@@ -154,87 +194,114 @@
     in_hi_x = (gx < ngx - 1).astype(F32)
     in_lo_y = (yz > 0).astype(F32)
     in_hi_y = (yz < nyz - 1).astype(F32)
-
-    for copy in waits:
+    terms = cheb_terms()
+
+    for copy in y_waits + c_waits + x_waits:
         copy.wait_recv()
 
-    terms = [(None, 1.0 / THETA)] + cheb_terms()
-
-    def spread(x_at, below, above, w):
-        x = x_at(0)
-        up, down = y_beside(x, below, above)
+    sub = rows((8, NZ))
+    for side, start, fifth in ((0, 0, 3), (1, PY + NY, 4)):
+        tile = pl.ds(start, 8)
+        inside = in_lo_y if side == 0 else in_hi_y
+        for p in range(NX):
+            a = rk[side, tile_a(p)] * inside
+            deep = rk[side, 16, p : p + 1, :] * inside
+            xa[PX + p, tile, :] = jnp.where(sub == fifth, jnp.broadcast_to(deep, a.shape), a)
+            deep = rk[side, 17, p : p + 1, :] * inside
+            be[PX + p, tile, :] = jnp.where(sub == fifth, jnp.broadcast_to(deep, a.shape), pltpu.roll(a, 4, 0))
+            b = rk[side, tile_b(p)]
+            al[PX + p, tile, :] = b
+            rh[PX + p, tile, :] = pltpu.roll(b, 4, 0)
+        for sx in (0, 1):
+            shift = 9 if sx == 0 else 0
+            for p in range(4, 8) if sx == 0 else range(4):
+                plane = PX + p - NX if sx == 0 else PX + p + NX
+                a = rc[sx, side, tile_a(p) - shift] * inside
+                xa[plane, tile, :] = a
+                be[plane, tile, :] = pltpu.roll(a, 4, 0)
+                if p not in (3, 4):
+                    b = rc[sx, side, tile_b(p) - shift]
+                    al[plane, tile, :] = b
+                    rh[plane, tile, :] = pltpu.roll(b, 4, 0)
+
+    for edge, start in ((gx == 0, 0), (gx == ngx - 1, PX + NX)):
+
+        @pl.when(edge)
+        def _(start=start):
+            for plane in range(start, start + DEPTH):
+                xa[plane] = jnp.zeros((EY, NZ), F32)
+                be[plane] = jnp.zeros((EY, NZ), F32)
+
+    def fine_blocks(deep):
+        found = []
+        for p in range(-deep, NX + deep):
+            beyond = max(-p, p - NX + 1, 0)
+            found.append((p, (0, EY) if beyond < deep else (PY, PY + NY)))
+        return found
+
+    def spread(x, x_at, span, w):
+        if span == (0, EY):
+            up, down = pltpu.roll(x, EY - 1, 0), pltpu.roll(x, 1, 0)
+        else:
+            up, down = y_beside(x, x_at(0, (PY - 1, PY)), x_at(0, (PY + NY, PY + NY + 1)))
         right, left = z_beside(x)
         return (
-            w(0) * x_at(1) + w(1) * x_at(-1) + w(2) * up + w(3) * down + w(4) * right + w(5) * left
-        )
-
-    lane = lanes((NY, NZ))
-    row = rows((NY, NZ))
-    for p in range(NX):
-        b = gb[1, p]
-        b_hi = gb[1, p + 1] if p < NX - 1 else hx0[1, 1] * in_hi_x
-        b_lo = gb[1, p - 1] if p > 0 else hx0[0, 1] * in_lo_x
-        b_up, b_down = y_beside(
-            b, hy0[0, 1, p : p + 1, :] * in_lo_y, hy0[1, 1, p : p + 1, :] * in_hi_y
-        )
+            w(0) * x_at(1, span) + w(1) * x_at(-1, span) + w(2) * up + w(3) * down + w(4) * right + w(5) * left
+        )
+
+    for p, span in fine_blocks(DEPTH - 1):
+        lo, hi = span
+        here = pl.ds(lo, hi - lo)
+        shape = (hi - lo, NZ)
+        lane = lanes(shape)
+        b = be[PX + p, here, :]
+        if span == (0, EY):
+            b_up, b_down = pltpu.roll(b, EY - 1, 0), pltpu.roll(b, 1, 0)
+        else:
+            b_up, b_down = y_beside(b, be[PX + p, PY - 1 : PY, :], be[PX + p, PY + NY : PY + NY + 1, :])
         b_right, b_left = z_beside(b)
         b_right = jnp.where(lane == NZ - 1, 0.0, b_right)
         b_left = jnp.where(lane == 0, 0.0, b_left)
-        faces = [0.5 * (b + other) for other in (b_hi, b_lo, b_up, b_down, b_right, b_left)]
+        faces = [
+            0.5 * (b + other)
+            for other in (be[PX + p + 1, here, :], be[PX + p - 1, here, :], b_up, b_down, b_right, b_left)
+        ]
         total = faces[0] + faces[1] + faces[2] + faces[3] + faces[4] + faces[5]
-        whole = alpha[p] + total
-        diag[p] = whole
+        whole = al[PX + p, here, :] + total
+        if 0 <= p < NX:
+            diag[p] = whole[PY - lo : PY - lo + NY]
         inverse = 1.0 / whole
+        if p < 0:
+            inverse = inverse * in_lo_x
+        if p >= NX:
+            inverse = inverse * in_hi_x
+        if span == (0, EY):
+            row = rows(shape)
+            inside = jnp.where(row < PY, in_lo_y, jnp.where(row >= PY + NY, in_hi_y, 1.0))
+            inverse = inverse * inside
         w = [inverse * face for face in faces]
-        if p == NX - 1:
-            w[0] = w[0] * in_hi_x
-        if p == 0:
-            w[1] = w[1] * in_lo_x
-        w[2] = jnp.where(row == NY - 1, w[2] * in_hi_y, w[2])
-        w[3] = jnp.where(row == 0, w[3] * in_lo_y, w[3])
         w[4] = jnp.where(lane == NZ - 1, 0.0, w[4])
         w[5] = jnp.where(lane == 0, 0.0, w[5])
         for e in range(6):
-            ws[e, p] = w[e]
-        g = inverse * rhs[p]
-        gs[p] = g
-
-        def x_at(step, p=p):
-            if p + step < 0:
-                return hx0[0, 0]
-            if p + step >= NX:
-                return hx0[1, 0]
-            return gb[0, p + step]
-
-        x = gb[0, p]
-        resid = g - x + spread(x_at, hy0[0, 0, p : p + 1, :], hy0[1, 0, p : p + 1, :], lambda e: w[e])
+            ws[e, PX + p, here, :] = w[e]
+        g = inverse * rh[PX + p, here, :]
+        gs[PX + p, here, :] = g
+        x = xa[PX + p, here, :]
+        resid = g - x + spread(x, lambda step, part: xa[PX + p + step, part[0] : part[1], :], span, lambda e: w[e])
         update = resid * (1.0 / THETA)
-        ds[p] = update
-        xs[0, p] = x + update
-
-    def post(r, cur):
-        for p in range(NX):
-            sy[r, 0, p : p + 1, :] = xs[cur, p, NY - 1 : NY, :]
-            sy[r, 1, p : p + 1, :] = xs[cur, p, 0:1, :]
-        return [
-            send(sy.at[r, 0], hy.at[r, 0], sy_sem.at[r + 1, 0], ry_sem.at[r + 1, 0], at(0, 1)),
-            send(sy.at[r, 1], hy.at[r, 1], sy_sem.at[r + 1, 1], ry_sem.at[r + 1, 1], at(0, -1)),
-            send(xs.at[cur, NX - 1], hx.at[r, 0], sx_sem.at[r + 1, 0], rx_sem.at[r + 1, 0], at(1, 0)),
-            send(xs.at[cur, 0], hx.at[r, 1], sx_sem.at[r + 1, 1], rx_sem.at[r + 1, 1], at(-1, 0)),
-        ]
-
-    def residual(r, cur, p):
-        def x_at(step):
-            if p + step < 0:
-                return hx[r, 0]
-            if p + step >= NX:
-                return hx[r, 1]
-            return xs[cur, p + step]
-
+        ds[PX + p, here, :] = update
+        xb[PX + p, here, :] = x + update
+
+    def residual(cur, p, span):
+        here = pl.ds(span[0], span[1] - span[0])
+        x = cur[PX + p, here, :]
         return (
-            gs[p]
-            - xs[cur, p]
-            + spread(x_at, hy[r, 0, p : p + 1, :], hy[r, 1, p : p + 1, :], lambda e: ws[e, p])
+            gs[PX + p, here, :]
+            - x
+            + spread(
+                x, lambda step, part: cur[PX + p + step, part[0] : part[1], :], span,
+                lambda e: ws[e, PX + p, here, :],
+            )
         )
 
     slot_in_x = (in_lo_x, None, in_hi_x)
@@ -265,13 +332,13 @@
                 found.append((plane, i, q, j))
         return found
 
-    def coarse_setup():
+    def coarse_setup(own_only):
         clane = lanes((CY, CZ))
 
         def beta(i, j, q):
             return masked(cab[i, j, 1, q], i, j)
 
-        for plane, i, q, j in coarse_slots(3):
+        for plane, i, q, j in coarse_slots(0 if own_only else 3):
             b = beta(i, j, q)
             hi, lo = plane + 1 + CX, plane - 1 + CX
             b_hi = beta(hi // CX, j, hi % CX)
@@ -283,8 +350,9 @@
             faces = [0.5 * (b + other) for other in (b_hi, b_lo, b_up, b_down, b_right, b_left)]
             total = faces[0] + faces[1] + faces[2] + faces[3] + faces[4] + faces[5]
             whole = cab[i, j, 0, q] + 0.25 * total
-            if (i, j) == (1, 1):
+            if own_only:
                 cdiag[q] = whole
+                continue
             scale = masked(0.25 / whole, i, j)
             w = [scale * face for face in faces]
             w[4] = jnp.where(clane == CZ - 1, 0.0, w[4])
@@ -292,37 +360,28 @@
             for e in range(6):
                 cw[e, i, j, q] = w[e]
 
-    cur = 0
-    for r in range(ROUNDS - 1):
-        round_waits = post(r, cur)
-        if r == 1:
-            for copy in ab_waits:
-                copy.wait_recv()
-            coarse_setup()
-        for copy in round_waits:
-            copy.wait_recv()
-        if r > 0:
-            for copy in earlier:
-                copy.wait_send()
-                done.append(id(copy))
-        earlier = round_waits[2:]
-        if r < ROUNDS - 2:
-            first, second = terms[r + 1]
-            for p in range(NX):
-                update = first * ds[p] + second * residual(r, cur, p)
-                ds[p] = update
-                xs[1 - cur, p] = xs[cur, p] + update
-            cur = 1 - cur
-        else:
-            for q in range(CX):
-                a = diag[2 * q] * residual(r, cur, 2 * q)
-                b = diag[2 * q + 1] * residual(r, cur, 2 * q + 1)
-                cg[1, 1, q] = 0.125 * restrict_pair(a, b) / cdiag[q]
+    cur, other = xb, xa
+    for step, (first, second) in enumerate(terms):
+        for p, span in fine_blocks(DEPTH - 2 - step):
+            here = pl.ds(span[0], span[1] - span[0])
+            update = first * ds[PX + p, here, :] + second * residual(cur, p, span)
+            ds[PX + p, here, :] = update
+            other[PX + p, here, :] = cur[PX + p, here, :] + update
+        cur, other = other, cur
+    own = (PY, PY + NY)
+    for copy in ab_waits:
+        copy.wait_recv()
+    coarse_setup(True)
+    for q in range(CX):
+        a = diag[2 * q] * residual(cur, 2 * q, own)
+        b = diag[2 * q + 1] * residual(cur, 2 * q + 1, own)
+        cg[1, 1, q] = 0.125 * restrict_pair(a, b) / cdiag[q]
 
     g_waits = [
         send(cg.at[1, 1], cg.at[1 - dx, 1 - dy], sg_sem.at[k], rg_sem.at[k], at(dx, dy))
         for k, (dx, dy) in enumerate(around)
     ]
+    coarse_setup(False)
     for copy in g_waits:
         copy.wait_recv()
 
@@ -383,7 +442,7 @@
             wide[t, pl.ds(1, CY, 2), :] = part
         full = jnp.concatenate([wide[t] for t in range(4)], axis=1)
         for p in (2 * q, 2 * q + 1):
-            out_ref[p] = xs[cur, p] + full
+            out_ref[p] = cur[PX + p, own_y, :] + full
 
     for copy in l_waits:
         copy.wait_recv()
@@ -391,26 +450,26 @@
         owner = lax.rem(gx + ngx - dx, ngx)
         last_ref[pl.ds(2 * owner, 2)] = coarsest[dx]
     for copy in sent:
-        if id(copy) not in done:
-            copy.wait_send()
+        copy.wait_send()
 
 
 def on_device(guess, rhs, alpha, beta):
     vmem = pltpu.VMEM
     dma = pltpu.SemaphoreType.DMA
     fine = (NX, NY, NZ)
+    wide = (EX, EY, NZ)
     scratch = [
-        vmem((2, *fine), F32), vmem(fine, F32), vmem(fine, F32), vmem((2, *fine), F32), vmem(fine, F32),
-        vmem(fine, F32), vmem(fine, F32), vmem((6, *fine), F32),
-        vmem((ROUNDS - 1, 2, NY, NZ), F32), vmem((ROUNDS - 1, 2, NX, NZ), F32), vmem((ROUNDS - 1, 2, NX, NZ), F32),
-        vmem((2, 2, NY, NZ), F32), vmem((2, 2, NX, NZ), F32), vmem((2, 2, NX, NZ), F32),
+        vmem(wide, F32), vmem(wide, F32), vmem(wide, F32), vmem(wide, F32), vmem(wide, F32), vmem(wide, F32),
+        vmem(wide, F32), vmem(fine, F32), vmem((6, *wide), F32),
+        vmem((2, 18, 8, NZ), F32), vmem((2, 18, 8, NZ), F32), vmem((2, 2, 7, 8, NZ), F32),
         vmem((4, NY, 128), F32), vmem((4, NY, 128), F32),
         vmem((3, 3, 2, CX, CY, CZ), F32), vmem((3, 3, CX, CY, CZ), F32), vmem((6, 3, 3, CX, CY, CZ), F32),
         vmem((2, 3, 3, CX, CY, CZ), F32), vmem((3, 3, CX, CY, CZ), F32), vmem((CX, CY, CZ), F32),
         vmem((8, 2, CY // 2, CZ // 2), F32),
-        dma((4,)), dma((ROUNDS, 2)), dma((ROUNDS, 2)), dma((ROUNDS, 2)), dma((ROUNDS, 2)),
+        dma((4,)), dma((4, 2)), dma((4, 2)), dma((2,)), dma((2,)), dma((2, 2)), dma((2, 2)),
         dma((8,)), dma((8,)), dma((8,)), dma((8,)), dma((8,)), dma((8,)),
     ]
+    placed = [pltpu.with_memory_space_constraint(x, pltpu.HBM) for x in (guess, rhs, alpha, beta)]
     return pl.pallas_call(
         kernel,
         out_shape=(
@@ -421,10 +480,10 @@
         out_specs=(pl.BlockSpec(memory_space=vmem), pl.BlockSpec(memory_space=vmem)),
         scratch_shapes=scratch,
         compiler_params=pltpu.CompilerParams(
-            collective_id=0, has_side_effects=True, vmem_limit_bytes=60 << 20
+            collective_id=0, has_side_effects=True, vmem_limit_bytes=40 << 20
         ),
         name="vcycle",
-    )(guess, rhs, alpha, beta)
+    )(*placed)
 
 
 def solution(mesh):

time: 48.9 us -> 43.8 us (0.90)
  Pallas kernels: 45.9 us -> 41.7 us
  local copies, waits for them, and re-layouts: 2.3 us -> 1.32 us
    pallas_call x1, Pallas kernels: 45.9 us -> 41.7 us  [on_device(): pl.pallas_call(kernel, out_shape=(jax.ShapeDtypeStruct(fine, F32), jax.Sh...]
    unnamed x4 -> x2, local copies, waits for them, and re-layouts: 2.3 us -> 1.32 us
where the time goes in v2:
time: 43.8 us; the launch traced here: 43.7 us
  Pallas kernels  41.7 us (95%)
  local copies, waits for them, and re-layouts  1.32 us (3%)
  between operations  0.64 us (1%)
    pallas_call x1, Pallas kernels, on_device(): pl.pallas_call(kernel, out_shape=(jax.ShapeDtypeStruct(fine, F32), jax.Sh...  41.7 us
    unnamed x2, local copies, waits for them, and re-layouts  1.32 us

profile of v2, /device:TPU:1, one launch (start us, length us, event | category | flops | bytes accessed | tf_op | source)
XLA Modules:
  0.0 43.7 jit_solution(6291193135579196042)
XLA Ops:
  0.6 41.7 %vcycle.1 = (f32[8,16,512]{2,1,0:T(8,128)S(1)}, f32[16,4,128]{2,1,0:T(4,128)S(1)}) custom-call(f32[8,16,512]{2,1,0:T(8,128)} %guess_h.1, f32[8,16,512]{2,1,0:T(8,128)} %rhs_h.1, f32[8,16,512]{2,1,0:T(8,128)} %alpha_h.1, f32[8,16,512]{2,1,0:T(8,128)} %beta_h.1), custom_call_target="tpu_custom_call" | custom-call | tf_op jit(solution)/shard_map/vcycle/pallas_call | solution.py:473
  42.3 0.7 %copy.8 = f32[8,16,512]{2,1,0:T(8,128)} copy(f32[8,16,512]{2,1,0:T(8,128)S(1)} %get-tuple-element.4) | data formatting | bytes 524288
  43.0 0.6 %copy.9 = f32[16,4,128]{2,1,0:T(4,128)} copy(f32[16,4,128]{2,1,0:T(4,128)S(1)} %get-tuple-element.5) | data formatting | bytes 65536

commit v3 on v2

--- a/solution.py
+++ b/solution.py
@@ -101,12 +101,25 @@
     def at(dx, dy):
         return (lax.rem(gx + ngx + dx, ngx), lax.rem(yz + nyz + dy, nyz))
 
+    beside = {-1: yz > 0, 0: None, 1: yz < nyz - 1}
+
+    def when(condition, act):
+        if condition is None:
+            act()
+        else:
+            pl.when(condition)(act)
+
+    def greet(dx, dy):
+        pl.semaphore_signal(barrier, inc=1, device_id=at(dx, dy), device_id_type=MESH)
+
     around = [(dx, dy) for dx in (-1, 0, 1) for dy in (-1, 0, 1) if (dx, dy) != (0, 0)]
-    peers = [(dx, 0) for dx in range(1, 8)]
-    greet = [at(dx, dy) for dx, dy in peers] + [at(dx, dy) for dx, dy in around if dy != 0]
     barrier = pltpu.get_barrier_semaphore()
-    for device in greet:
-        pl.semaphore_signal(barrier, inc=1, device_id=device, device_id_type=MESH)
+    for dx in range(1, 8):
+        greet(dx, 0)
+    for dx, dy in around:
+        if dy != 0:
+            when(beside[dy], functools.partial(greet, dx, dy))
+    greeted = 7 + 3 * (yz > 0).astype(jnp.int32) + 3 * (yz < nyz - 1).astype(jnp.int32)
 
     own_x, own_y = pl.ds(PX, NX), pl.ds(PY, NY)
     loads = []
@@ -130,31 +143,56 @@
             pk[side, tile_b(p)] = packed(al[PX + p, tile, :], rh[PX + p, tile, :], side)
             pk[side, 16, p : p + 1, :] = xa[PX + p, fifth : fifth + 1, :]
             pk[side, 17, p : p + 1, :] = be[PX + p, fifth : fifth + 1, :]
-    pl.semaphore_wait(barrier, len(greet))
-
-    sent = []
-
-    def send(src, dst, s_sem, r_sem, device):
-        copy = pltpu.make_async_remote_copy(
+    for side, missing in ((0, yz == 0), (1, yz == nyz - 1)):
+
+        @pl.when(missing)
+        def _(side=side):
+            rk[side] = jnp.ones(rk.shape[1:], F32)
+            for k in range(3):
+                if k < 2:
+                    rc[k, side] = jnp.ones(rc.shape[2:], F32)
+                cab[k, 2 * side] = jnp.ones(cab.shape[2:], F32)
+                cg[k, 2 * side] = jnp.ones(cg.shape[2:], F32)
+
+    pl.semaphore_wait(barrier, greeted)
+
+    sent, corners_sent = [], []
+
+    def copy_of(src, dst, s_sem, r_sem, device):
+        return pltpu.make_async_remote_copy(
             src_ref=src, dst_ref=dst, send_sem=s_sem, recv_sem=r_sem, device_id=device, device_id_type=MESH
         )
-        copy.start()
-        sent.append(copy)
-        return copy
+
+    def send(src, dst, s_sem, r_sem, dx, dy):
+        copy = copy_of(src, dst, s_sem, r_sem, at(dx, dy))
+        when(beside[dy], copy.start)
+        sent.append((copy, dy))
+        return copy, dy
+
+    def wait_for(copies):
+        for copy, dy in copies:
+            when(beside[-dy], copy.wait_recv)
 
     y_waits = [
-        send(pk.at[side], rk.at[side], sy_sem.at[side], ry_sem.at[side], at(0, 1 - 2 * side)) for side in (0, 1)
+        send(pk.at[side], rk.at[side], sy_sem.at[side], ry_sem.at[side], 0, 1 - 2 * side) for side in (0, 1)
     ]
-    c_waits = []
+    first_core = lax.rem(gx, 2) == 0
+    c_waits, relays = [], ([], [])
     for sx in (0, 1):
+        part = pl.ds(9, 7) if sx == 0 else pl.ds(0, 7)
+        same_chip = first_core if sx == 0 else jnp.logical_not(first_core)
         for sy in (0, 1):
-            part = pl.ds(9, 7) if sx == 0 else pl.ds(0, 7)
-            c_waits.append(
-                send(
-                    pk.at[sy, part], rc.at[sx, sy], sc_sem.at[sx, sy], rc_sem.at[sx, sy],
-                    at(1 - 2 * sx, 1 - 2 * sy),
-                )
+            dy = 1 - 2 * sy
+            sems = (sc_sem.at[sx, sy], rc_sem.at[sx, sy])
+            straight = copy_of(pk.at[sy, part], rc.at[sx, sy], *sems, at(1 - 2 * sx, dy))
+            relay = copy_of(rk.at[sy, part], rc.at[sx, sy], *sems, at(1 - 2 * sx, 0))
+            pl.when(jnp.logical_and(jnp.logical_not(same_chip), beside[dy]))(straight.start)
+            relays[sy].append((relay, jnp.logical_and(same_chip, beside[-dy])))
+            c_waits.append((straight, dy))
+            gone = jnp.logical_or(
+                jnp.logical_and(same_chip, beside[-dy]), jnp.logical_and(jnp.logical_not(same_chip), beside[dy])
             )
+            corners_sent.append((straight, gone))
     x_waits = []
     for k, (src, dst, deep) in enumerate(
         ((guess_h, xa, DEPTH), (beta_h, be, DEPTH), (alpha_h, al, DEPTH - 1), (rhs_h, rh, DEPTH - 1))
@@ -162,13 +200,13 @@
         x_waits.append(
             send(
                 src.at[pl.ds(NX - deep, deep)], dst.at[pl.ds(PX - deep, deep), own_y],
-                sx_sem.at[k, 0], rx_sem.at[k, 0], at(1, 0),
+                sx_sem.at[k, 0], rx_sem.at[k, 0], 1, 0,
             )
         )
         x_waits.append(
             send(
                 src.at[pl.ds(0, deep)], dst.at[pl.ds(PX + NX, deep), own_y],
-                sx_sem.at[k, 1], rx_sem.at[k, 1], at(-1, 0),
+                sx_sem.at[k, 1], rx_sem.at[k, 1], -1, 0,
             )
         )
 
@@ -186,7 +224,7 @@
         cab[1, 1, 0, q] = 0.125 * restrict_pair(al[one, own_y, :], al[two, own_y, :])
         cab[1, 1, 1, q] = 0.125 * restrict_pair(be[one, own_y, :], be[two, own_y, :])
     ab_waits = [
-        send(cab.at[1, 1], cab.at[1 - dx, 1 - dy], sab_sem.at[k], rab_sem.at[k], at(dx, dy))
+        send(cab.at[1, 1], cab.at[1 - dx, 1 - dy], sab_sem.at[k], rab_sem.at[k], dx, dy)
         for k, (dx, dy) in enumerate(around)
     ]
 
@@ -196,41 +234,43 @@
     in_hi_y = (yz < nyz - 1).astype(F32)
     terms = cheb_terms()
 
-    for copy in y_waits + c_waits + x_waits:
-        copy.wait_recv()
-
     sub = rows((8, NZ))
-    for side, start, fifth in ((0, 0, 3), (1, PY + NY, 4)):
-        tile = pl.ds(start, 8)
-        inside = in_lo_y if side == 0 else in_hi_y
-        for p in range(NX):
-            a = rk[side, tile_a(p)] * inside
-            deep = rk[side, 16, p : p + 1, :] * inside
-            xa[PX + p, tile, :] = jnp.where(sub == fifth, jnp.broadcast_to(deep, a.shape), a)
-            deep = rk[side, 17, p : p + 1, :] * inside
-            be[PX + p, tile, :] = jnp.where(sub == fifth, jnp.broadcast_to(deep, a.shape), pltpu.roll(a, 4, 0))
-            b = rk[side, tile_b(p)]
-            al[PX + p, tile, :] = b
-            rh[PX + p, tile, :] = pltpu.roll(b, 4, 0)
-        for sx in (0, 1):
-            shift = 9 if sx == 0 else 0
-            for p in range(4, 8) if sx == 0 else range(4):
-                plane = PX + p - NX if sx == 0 else PX + p + NX
-                a = rc[sx, side, tile_a(p) - shift] * inside
-                xa[plane, tile, :] = a
-                be[plane, tile, :] = pltpu.roll(a, 4, 0)
-                if p not in (3, 4):
-                    b = rc[sx, side, tile_b(p) - shift]
-                    al[plane, tile, :] = b
-                    rh[plane, tile, :] = pltpu.roll(b, 4, 0)
-
-    for edge, start in ((gx == 0, 0), (gx == ngx - 1, PX + NX)):
-
-        @pl.when(edge)
-        def _(start=start):
-            for plane in range(start, start + DEPTH):
-                xa[plane] = jnp.zeros((EY, NZ), F32)
-                be[plane] = jnp.zeros((EY, NZ), F32)
+    sides = ((0, 0, 3, in_lo_y), (1, PY + NY, 4, in_hi_y))
+
+    def place_rows():
+        for side, start, fifth, inside in sides:
+            tile = pl.ds(start, 8)
+            for p in range(NX):
+                a = rk[side, tile_a(p)] * inside
+                deep = rk[side, 16, p : p + 1, :] * inside
+                xa[PX + p, tile, :] = jnp.where(sub == fifth, jnp.broadcast_to(deep, a.shape), a)
+                deep = rk[side, 17, p : p + 1, :] * inside
+                be[PX + p, tile, :] = jnp.where(sub == fifth, jnp.broadcast_to(deep, a.shape), pltpu.roll(a, 4, 0))
+                b = rk[side, tile_b(p)]
+                al[PX + p, tile, :] = b
+                rh[PX + p, tile, :] = pltpu.roll(b, 4, 0)
+
+    def place_corners():
+        for side, start, _, inside in sides:
+            tile = pl.ds(start, 8)
+            for sx in (0, 1):
+                shift = 9 if sx == 0 else 0
+                for p in range(4, 8) if sx == 0 else range(4):
+                    plane = PX + p - NX if sx == 0 else PX + p + NX
+                    a = rc[sx, side, tile_a(p) - shift] * inside
+                    xa[plane, tile, :] = a
+                    be[plane, tile, :] = pltpu.roll(a, 4, 0)
+                    if p not in (3, 4):
+                        b = rc[sx, side, tile_b(p) - shift]
+                        al[plane, tile, :] = b
+                        rh[plane, tile, :] = pltpu.roll(b, 4, 0)
+        for edge, start in ((gx == 0, 0), (gx == ngx - 1, PX + NX)):
+
+            @pl.when(edge)
+            def _(start=start):
+                for plane in range(start, start + DEPTH):
+                    xa[plane] = jnp.zeros((EY, NZ), F32)
+                    be[plane] = jnp.zeros((EY, NZ), F32)
 
     def fine_blocks(deep):
         found = []
@@ -249,7 +289,7 @@
             w(0) * x_at(1, span) + w(1) * x_at(-1, span) + w(2) * up + w(3) * down + w(4) * right + w(5) * left
         )
 
-    for p, span in fine_blocks(DEPTH - 1):
+    def first_step(p, span):
         lo, hi = span
         here = pl.ds(lo, hi - lo)
         shape = (hi - lo, NZ)
@@ -360,17 +400,37 @@
             for e in range(6):
                 cw[e, i, j, q] = w[e]
 
-    cur, other = xb, xa
-    for step, (first, second) in enumerate(terms):
-        for p, span in fine_blocks(DEPTH - 2 - step):
-            here = pl.ds(span[0], span[1] - span[0])
-            update = first * ds[PX + p, here, :] + second * residual(cur, p, span)
-            ds[PX + p, here, :] = update
-            other[PX + p, here, :] = cur[PX + p, here, :] + update
-        cur, other = other, cur
+    def later_step(step, p, span):
+        cur, other = (xb, xa) if step % 2 == 1 else (xa, xb)
+        first, second = terms[step - 1]
+        here = pl.ds(span[0], span[1] - span[0])
+        update = first * ds[PX + p, here, :] + second * residual(cur, p, span)
+        ds[PX + p, here, :] = update
+        other[PX + p, here, :] = cur[PX + p, here, :] + update
+
+    def fine_step(step, chosen):
+        for p, span in fine_blocks(DEPTH - 1 - step):
+            if (1 + step <= p < NX - 1 - step) == chosen:
+                if step == 0:
+                    first_step(p, span)
+                else:
+                    later_step(step, p, span)
+
+    for side in (0, 1):
+        wait_for(y_waits[side : side + 1])
+        for relay, passes in relays[side]:
+            pl.when(passes)(relay.start)
+    place_rows()
+    for step in range(DEGREE):
+        fine_step(step, True)
+    wait_for(x_waits)
+    wait_for(c_waits)
+    place_corners()
+    for step in range(DEGREE):
+        fine_step(step, False)
+    cur = xa if DEGREE % 2 == 0 else xb
     own = (PY, PY + NY)
-    for copy in ab_waits:
-        copy.wait_recv()
+    wait_for(ab_waits)
     coarse_setup(True)
     for q in range(CX):
         a = diag[2 * q] * residual(cur, 2 * q, own)
@@ -378,12 +438,11 @@
         cg[1, 1, q] = 0.125 * restrict_pair(a, b) / cdiag[q]
 
     g_waits = [
-        send(cg.at[1, 1], cg.at[1 - dx, 1 - dy], sg_sem.at[k], rg_sem.at[k], at(dx, dy))
+        send(cg.at[1, 1], cg.at[1 - dx, 1 - dy], sg_sem.at[k], rg_sem.at[k], dx, dy)
         for k, (dx, dy) in enumerate(around)
     ]
     coarse_setup(False)
-    for copy in g_waits:
-        copy.wait_recv()
+    wait_for(g_waits)
 
     def coarse_g(i, j, q):
         return masked(cg[i, j, q], i, j)
@@ -431,7 +490,7 @@
         )
         coarsest[0, h] = 0.125 * halve_z(summed)
     l_waits = [
-        send(coarsest.at[0], coarsest.at[dx], sl_sem.at[dx], rl_sem.at[dx], at(dx, 0)) for dx in range(1, 8)
+        send(coarsest.at[0], coarsest.at[dx], sl_sem.at[dx], rl_sem.at[dx], dx, 0) for dx in range(1, 8)
     ]
 
     for q in range(CX):
@@ -444,13 +503,14 @@
         for p in (2 * q, 2 * q + 1):
             out_ref[p] = cur[PX + p, own_y, :] + full
 
-    for copy in l_waits:
-        copy.wait_recv()
+    wait_for(l_waits)
     for dx in range(8):
         owner = lax.rem(gx + ngx - dx, ngx)
         last_ref[pl.ds(2 * owner, 2)] = coarsest[dx]
-    for copy in sent:
-        copy.wait_send()
+    for copy, dy in sent:
+        when(beside[dy], copy.wait_send)
+    for copy, gone in corners_sent:
+        pl.when(gone)(copy.wait_send)
 
 
 def on_device(guess, rhs, alpha, beta):

time: 43.8 us -> 36.9 us (0.84)
  the two profiles are of different devices: /device:TPU:1 before, /device:TPU:7 now
where the time goes in v3:
time: 36.9 us; the launch traced here: 36.8 us
  Pallas kernels  34.8 us (94%)
  local copies, waits for them, and re-layouts  1.32 us (4%)
  between operations  0.64 us (2%)
    pallas_call x1, Pallas kernels, on_device(): pl.pallas_call(kernel, out_shape=(jax.ShapeDtypeStruct(fine, F32), jax.Sh...  34.8 us
    unnamed x2, local copies, waits for them, and re-layouts  1.32 us

profile of v3, /device:TPU:7, one launch (start us, length us, event | category | flops | bytes accessed | tf_op | source)
XLA Modules:
  0.0 36.8 jit_solution(866426786419519781)
XLA Ops:
  0.6 34.8 %vcycle.1 = (f32[8,16,512]{2,1,0:T(8,128)S(1)}, f32[16,4,128]{2,1,0:T(4,128)S(1)}) custom-call(f32[8,16,512]{2,1,0:T(8,128)} %guess_h.1, f32[8,16,512]{2,1,0:T(8,128)} %rhs_h.1, f32[8,16,512]{2,1,0:T(8,128)} %alpha_h.1, f32[8,16,512]{2,1,0:T(8,128)} %beta_h.1), custom_call_target="tpu_custom_call" | custom-call | tf_op jit(solution)/shard_map/vcycle/pallas_call | solution.py:533
  35.4 0.7 %copy.8 = f32[8,16,512]{2,1,0:T(8,128)} copy(f32[8,16,512]{2,1,0:T(8,128)S(1)} %get-tuple-element.4) | data formatting | bytes 524288
  36.1 0.6 %copy.9 = f32[16,4,128]{2,1,0:T(4,128)} copy(f32[16,4,128]{2,1,0:T(4,128)S(1)} %get-tuple-element.5) | data formatting | bytes 65536

commit v4 on v3

--- a/solution.py
+++ b/solution.py
@@ -16,8 +16,9 @@
 NX, NY, NZ = 8, 16, 512
 CX, CY, CZ = 4, 8, 256
 DEPTH = DEGREE + 1
-PX, PY = DEPTH, 8
-EX, EY = NX + 2 * DEPTH, NY + 2 * PY
+PX = DEPTH
+EX, EY = NX + 2 * DEPTH, NY + 8
+EXC, EYC = CX + 2 * DEGREE, CY + 8
 
 
 def cheb_terms():
@@ -90,7 +91,7 @@
 def kernel(
     guess_h, rhs_h, alpha_h, beta_h, out_ref, last_ref,
     xa, xb, be, al, rh, ds, gs, diag, ws, pk, rk, rc,
-    pair, wide, cab, cg, cw, cxs, cds, cdiag, coarsest,
+    pair, wide, cab, cg, pkc, rkc, cw, cxs, cds, cdiag, coarsest,
     load_sem, sx_sem, rx_sem, sy_sem, ry_sem, sc_sem, rc_sem, sab_sem, rab_sem, sg_sem, rg_sem, sl_sem, rl_sem,
 ):
     gx = lax.axis_index("gx")
@@ -121,7 +122,7 @@
             when(beside[dy], functools.partial(greet, dx, dy))
     greeted = 7 + 3 * (yz > 0).astype(jnp.int32) + 3 * (yz < nyz - 1).astype(jnp.int32)
 
-    own_x, own_y = pl.ds(PX, NX), pl.ds(PY, NY)
+    own_x, own_y, edge_y = pl.ds(PX, NX), pl.ds(0, NY), pl.ds(NY, 8)
     loads = []
     for k, (src, dst) in enumerate(((guess_h, xa), (beta_h, be), (alpha_h, al), (rhs_h, rh))):
         copy = pltpu.make_async_copy(src, dst.at[own_x, own_y], load_sem.at[k])
@@ -136,7 +137,7 @@
         moved = pltpu.roll(second, 4, 0)
         return jnp.where(half, moved, first) if side == 0 else jnp.where(half, first, moved)
 
-    for side, start, fifth in ((0, PY + 8, PY + 11), (1, PY, PY + 4)):
+    for side, start, fifth in ((0, 8, 11), (1, 0, 4)):
         tile = pl.ds(start, 8)
         for p in range(NX):
             pk[side, tile_a(p)] = packed(xa[PX + p, tile, :], be[PX + p, tile, :], side)
@@ -151,8 +152,8 @@
             for k in range(3):
                 if k < 2:
                     rc[k, side] = jnp.ones(rc.shape[2:], F32)
-                cab[k, 2 * side] = jnp.ones(cab.shape[2:], F32)
-                cg[k, 2 * side] = jnp.ones(cg.shape[2:], F32)
+                for f in range(3):
+                    rkc[f, k, side] = jnp.ones(rkc.shape[3:], F32)
 
     pl.semaphore_wait(barrier, greeted)
 
@@ -219,14 +220,36 @@
         )
         return halve_z(summed)
 
+    chalf = rows((8, CZ)) < 4
+
+    def pack_coarse(f, get):
+        for q in range(0, CX, 2):
+            this, then = get(q), pltpu.roll(get(q + 1), 4, 0)
+            pkc[f, 0, q // 2] = jnp.where(chalf, then, this)
+            pkc[f, 1, q // 2] = jnp.where(chalf, this, then)
+
+    def exchange_coarse(fields, own, others, s_sem, r_sem):
+        copies = []
+        for k, (dx, dy) in enumerate(around):
+            if dy == 0:
+                src, dst = own, others[1 - dx]
+            else:
+                side = (1 - dy) // 2
+                src, dst = pkc.at[fields, side], rkc.at[fields, 1 - dx, side]
+            copies.append(send(src, dst, s_sem.at[k], r_sem.at[k], dx, dy))
+        return copies
+
     for q in range(CX):
         one, two = PX + 2 * q, PX + 2 * q + 1
-        cab[1, 1, 0, q] = 0.125 * restrict_pair(al[one, own_y, :], al[two, own_y, :])
-        cab[1, 1, 1, q] = 0.125 * restrict_pair(be[one, own_y, :], be[two, own_y, :])
-    ab_waits = [
-        send(cab.at[1, 1], cab.at[1 - dx, 1 - dy], sab_sem.at[k], rab_sem.at[k], dx, dy)
-        for k, (dx, dy) in enumerate(around)
-    ]
+        cab[0, CX + q, 0:CY] = 0.125 * restrict_pair(al[one, own_y, :], al[two, own_y, :])
+        cab[1, CX + q, 0:CY] = 0.125 * restrict_pair(be[one, own_y, :], be[two, own_y, :])
+    for f in range(2):
+        pack_coarse(f, lambda q, f=f: cab[f, CX + q, 0:CY])
+    slots = [pl.ds(k * CX, CX) for k in range(3)]
+    ab_waits = exchange_coarse(
+        pl.ds(0, 2), cab.at[:, slots[1], pl.ds(0, CY)],
+        [cab.at[:, slot, pl.ds(0, CY)] for slot in slots], sab_sem, rab_sem,
+    )
 
     in_lo_x = (gx > 0).astype(F32)
     in_hi_x = (gx < ngx - 1).astype(F32)
@@ -234,36 +257,28 @@
     in_hi_y = (yz < nyz - 1).astype(F32)
     terms = cheb_terms()
 
-    sub = rows((8, NZ))
-    sides = ((0, 0, 3, in_lo_y), (1, PY + NY, 4, in_hi_y))
+    def join(below, above):
+        return jnp.where(half, above, below)
+
+    def place(plane, a_below, a_above, b_below=None, b_above=None):
+        a_below, a_above = a_below * in_lo_y, a_above * in_hi_y
+        xa[plane, edge_y, :] = join(a_below, a_above)
+        be[plane, edge_y, :] = pltpu.roll(join(a_above, a_below), 4, 0)
+        if b_below is not None:
+            al[plane, edge_y, :] = join(b_below, b_above)
+            rh[plane, edge_y, :] = pltpu.roll(join(b_above, b_below), 4, 0)
 
     def place_rows():
-        for side, start, fifth, inside in sides:
-            tile = pl.ds(start, 8)
-            for p in range(NX):
-                a = rk[side, tile_a(p)] * inside
-                deep = rk[side, 16, p : p + 1, :] * inside
-                xa[PX + p, tile, :] = jnp.where(sub == fifth, jnp.broadcast_to(deep, a.shape), a)
-                deep = rk[side, 17, p : p + 1, :] * inside
-                be[PX + p, tile, :] = jnp.where(sub == fifth, jnp.broadcast_to(deep, a.shape), pltpu.roll(a, 4, 0))
-                b = rk[side, tile_b(p)]
-                al[PX + p, tile, :] = b
-                rh[PX + p, tile, :] = pltpu.roll(b, 4, 0)
+        for p in range(NX):
+            place(PX + p, rk[0, tile_a(p)], rk[1, tile_a(p)], rk[0, tile_b(p)], rk[1, tile_b(p)])
 
     def place_corners():
-        for side, start, _, inside in sides:
-            tile = pl.ds(start, 8)
-            for sx in (0, 1):
-                shift = 9 if sx == 0 else 0
-                for p in range(4, 8) if sx == 0 else range(4):
-                    plane = PX + p - NX if sx == 0 else PX + p + NX
-                    a = rc[sx, side, tile_a(p) - shift] * inside
-                    xa[plane, tile, :] = a
-                    be[plane, tile, :] = pltpu.roll(a, 4, 0)
-                    if p not in (3, 4):
-                        b = rc[sx, side, tile_b(p) - shift]
-                        al[plane, tile, :] = b
-                        rh[plane, tile, :] = pltpu.roll(b, 4, 0)
+        for sx in (0, 1):
+            shift = 9 if sx == 0 else 0
+            for p in range(4, 8) if sx == 0 else range(4):
+                plane = PX + p - NX if sx == 0 else PX + p + NX
+                tiles = [tile_a(p) - shift] if p in (3, 4) else [tile_a(p) - shift, tile_b(p) - shift]
+                place(plane, *(rc[sx, side, tile] for tile in tiles for side in (0, 1)))
         for edge, start in ((gx == 0, 0), (gx == ngx - 1, PX + NX)):
 
             @pl.when(edge)
@@ -276,18 +291,30 @@
         found = []
         for p in range(-deep, NX + deep):
             beyond = max(-p, p - NX + 1, 0)
-            found.append((p, (0, EY) if beyond < deep else (PY, PY + NY)))
+            found.append((p, (0, EY) if beyond < deep else (0, NY)))
         return found
 
-    def spread(x, x_at, span, w):
-        if span == (0, EY):
-            up, down = pltpu.roll(x, EY - 1, 0), pltpu.roll(x, 1, 0)
-        else:
-            up, down = y_beside(x, x_at(0, (PY - 1, PY)), x_at(0, (PY + NY, PY + NY + 1)))
+    def along_y(x, at_row, span, own, fifth=None):
+        count = own + 8
+        if span == (0, own):
+            return y_beside(x, at_row(count - 1), at_row(own))
+        up, down = pltpu.roll(x, count - 1, 0), pltpu.roll(x, 1, 0)
+        if fifth is not None:
+            row = rows(x.shape)
+            up = jnp.where(row == own + 3, jnp.broadcast_to(fifth[1], x.shape), up)
+            down = jnp.where(row == own + 4, jnp.broadcast_to(fifth[0], x.shape), down)
+        return up, down
+
+    def spread(x, x_at, span, own, w, fifth=None):
+        up, down = along_y(x, lambda row: x_at(0, (row, row + 1)), span, own, fifth)
         right, left = z_beside(x)
         return (
             w(0) * x_at(1, span) + w(1) * x_at(-1, span) + w(2) * up + w(3) * down + w(4) * right + w(5) * left
         )
+
+    def in_rows(shape, own):
+        row = rows(shape)
+        return jnp.where(row < own, 1.0, jnp.where(row < own + 4, in_hi_y, in_lo_y))
 
     def first_step(p, span):
         lo, hi = span
@@ -295,10 +322,12 @@
         shape = (hi - lo, NZ)
         lane = lanes(shape)
         b = be[PX + p, here, :]
-        if span == (0, EY):
-            b_up, b_down = pltpu.roll(b, EY - 1, 0), pltpu.roll(b, 1, 0)
-        else:
-            b_up, b_down = y_beside(b, be[PX + p, PY - 1 : PY, :], be[PX + p, PY + NY : PY + NY + 1, :])
+        fifth = fifth_b = None
+        if 0 <= p < NX:
+            part = slice(p, p + 1)
+            fifth = (rk[0, 16, part, :] * in_lo_y, rk[1, 16, part, :] * in_hi_y)
+            fifth_b = (rk[0, 17, part, :] * in_lo_y, rk[1, 17, part, :] * in_hi_y)
+        b_up, b_down = along_y(b, lambda row: be[PX + p, row : row + 1, :], span, NY, fifth_b)
         b_right, b_left = z_beside(b)
         b_right = jnp.where(lane == NZ - 1, 0.0, b_right)
         b_left = jnp.where(lane == 0, 0.0, b_left)
@@ -309,16 +338,14 @@
         total = faces[0] + faces[1] + faces[2] + faces[3] + faces[4] + faces[5]
         whole = al[PX + p, here, :] + total
         if 0 <= p < NX:
-            diag[p] = whole[PY - lo : PY - lo + NY]
+            diag[p] = whole[0:NY]
         inverse = 1.0 / whole
         if p < 0:
             inverse = inverse * in_lo_x
         if p >= NX:
             inverse = inverse * in_hi_x
         if span == (0, EY):
-            row = rows(shape)
-            inside = jnp.where(row < PY, in_lo_y, jnp.where(row >= PY + NY, in_hi_y, 1.0))
-            inverse = inverse * inside
+            inverse = inverse * in_rows(shape, NY)
         w = [inverse * face for face in faces]
         w[4] = jnp.where(lane == NZ - 1, 0.0, w[4])
         w[5] = jnp.where(lane == 0, 0.0, w[5])
@@ -327,7 +354,7 @@
         g = inverse * rh[PX + p, here, :]
         gs[PX + p, here, :] = g
         x = xa[PX + p, here, :]
-        resid = g - x + spread(x, lambda step, part: xa[PX + p + step, part[0] : part[1], :], span, lambda e: w[e])
+        resid = g - x + spread(x, lambda step, part: xa[PX + p + step, part[0] : part[1], :], span, NY, lambda e: w[e], fifth)
         update = resid * (1.0 / THETA)
         ds[PX + p, here, :] = update
         xb[PX + p, here, :] = x + update
@@ -339,66 +366,60 @@
             gs[PX + p, here, :]
             - x
             + spread(
-                x, lambda step, part: cur[PX + p + step, part[0] : part[1], :], span,
+                x, lambda step, part: cur[PX + p + step, part[0] : part[1], :], span, NY,
                 lambda e: ws[e, PX + p, here, :],
             )
         )
 
-    slot_in_x = (in_lo_x, None, in_hi_x)
-    slot_in_y = (in_lo_y, None, in_hi_y)
-
-    def slot_mask(i, j):
-        masks = [m for m in (slot_in_x[i], slot_in_y[j]) if m is not None]
-        if not masks:
-            return None
-        return masks[0] if len(masks) == 1 else masks[0] * masks[1]
-
-    def masked(value, i, j):
-        mask = slot_mask(i, j)
+    def coarse_blocks(deep):
+        found = []
+        for p in range(-deep, CX + deep):
+            beyond = max(-p, p - CX + 1, 0)
+            found.append((p, CX + p, (0, EYC) if beyond < deep else (0, CY)))
+        return found
+
+    def in_planes(p):
+        return in_lo_x if p < 0 else in_hi_x if p >= CX else None
+
+    def masked(value, mask):
         return value if mask is None else value * mask
 
-    def coarse_y(get, i, q, j):
-        here = get(i, j, q)
-        below = get(i, j - 1, q)[CY - 1 : CY, :] if j > 0 else here[0:1, :]
-        above = get(i, j + 1, q)[0:1, :] if j < 2 else here[CY - 1 : CY, :]
-        return y_beside(here, below, above)
-
-    def coarse_slots(depth):
-        found = []
-        for plane in range(-depth, CX + depth):
-            beyond = max(-plane, plane - CX + 1, 0)
-            i, q = (plane + CX) // CX, (plane + CX) % CX
-            for j in (0, 1, 2) if beyond < depth else (1,):
-                found.append((plane, i, q, j))
-        return found
+    def place_coarse(f, field, inside):
+        for k in range(3):
+            for q in range(0, CX, 2):
+                below, above = rkc[f, k, 0, q // 2], rkc[f, k, 1, q // 2]
+                if inside:
+                    below, above = below * in_lo_y, above * in_hi_y
+                field[k * CX + q, pl.ds(CY, 8), :] = jnp.where(chalf, above, below)
+                field[k * CX + q + 1, pl.ds(CY, 8), :] = pltpu.roll(jnp.where(chalf, below, above), 4, 0)
 
     def coarse_setup(own_only):
-        clane = lanes((CY, CZ))
-
-        def beta(i, j, q):
-            return masked(cab[i, j, 1, q], i, j)
-
-        for plane, i, q, j in coarse_slots(0 if own_only else 3):
-            b = beta(i, j, q)
-            hi, lo = plane + 1 + CX, plane - 1 + CX
-            b_hi = beta(hi // CX, j, hi % CX)
-            b_lo = beta(lo // CX, j, lo % CX)
-            b_up, b_down = coarse_y(beta, i, q, j)
+        for p, at_p, span in coarse_blocks(0 if own_only else 3):
+            here = pl.ds(0, span[1])
+            shape = (span[1], CZ)
+            clane = lanes(shape)
+            b = cab[1, at_p, here, :]
+            b_up, b_down = along_y(b, lambda row: cab[1, at_p, row : row + 1, :], span, CY)
             b_right, b_left = z_beside(b)
             b_right = jnp.where(clane == CZ - 1, 0.0, b_right)
             b_left = jnp.where(clane == 0, 0.0, b_left)
-            faces = [0.5 * (b + other) for other in (b_hi, b_lo, b_up, b_down, b_right, b_left)]
+            faces = [
+                0.5 * (b + other)
+                for other in (cab[1, at_p + 1, here, :], cab[1, at_p - 1, here, :], b_up, b_down, b_right, b_left)
+            ]
             total = faces[0] + faces[1] + faces[2] + faces[3] + faces[4] + faces[5]
-            whole = cab[i, j, 0, q] + 0.25 * total
+            whole = cab[0, at_p, here, :] + 0.25 * total
             if own_only:
-                cdiag[q] = whole
+                cdiag[p] = whole
                 continue
-            scale = masked(0.25 / whole, i, j)
+            scale = masked(0.25 / whole, in_planes(p))
+            if span == (0, EYC):
+                scale = scale * in_rows(shape, CY)
             w = [scale * face for face in faces]
             w[4] = jnp.where(clane == CZ - 1, 0.0, w[4])
             w[5] = jnp.where(clane == 0, 0.0, w[5])
             for e in range(6):
-                cw[e, i, j, q] = w[e]
+                cw[e, at_p, here, :] = w[e]
 
     def later_step(step, p, span):
         cur, other = (xb, xa) if step % 2 == 1 else (xa, xb)
@@ -429,58 +450,59 @@
     for step in range(DEGREE):
         fine_step(step, False)
     cur = xa if DEGREE % 2 == 0 else xb
-    own = (PY, PY + NY)
+    own = (0, NY)
     wait_for(ab_waits)
+    place_coarse(0, cab.at[0], False)
+    place_coarse(1, cab.at[1], True)
+    for p in (*range(-CX, 0), *range(CX, 2 * CX)):
+        cab[1, CX + p] = cab[1, CX + p] * in_planes(p)
     coarse_setup(True)
     for q in range(CX):
         a = diag[2 * q] * residual(cur, 2 * q, own)
         b = diag[2 * q + 1] * residual(cur, 2 * q + 1, own)
-        cg[1, 1, q] = 0.125 * restrict_pair(a, b) / cdiag[q]
-
-    g_waits = [
-        send(cg.at[1, 1], cg.at[1 - dx, 1 - dy], sg_sem.at[k], rg_sem.at[k], dx, dy)
-        for k, (dx, dy) in enumerate(around)
-    ]
+        cg[CX + q, 0:CY] = 0.125 * restrict_pair(a, b) / cdiag[q]
+
+    pack_coarse(2, lambda q: cg[CX + q, 0:CY])
+    g_waits = exchange_coarse(
+        2, cg.at[slots[1], pl.ds(0, CY)], [cg.at[slot, pl.ds(0, CY)] for slot in slots], sg_sem, rg_sem
+    )
     coarse_setup(False)
     wait_for(g_waits)
-
-    def coarse_g(i, j, q):
-        return masked(cg[i, j, q], i, j)
-
-    for plane, i, q, j in coarse_slots(4):
-        update = coarse_g(i, j, q) * (1.0 / THETA)
-        cxs[0, i, j, q] = update
-        cds[i, j, q] = update
-
-    def coarse_residual(now, plane, i, q, j):
-        def get(i, j, q):
-            return cxs[now, i, j, q]
-
-        x = get(i, j, q)
-        hi, lo = plane + 1 + CX, plane - 1 + CX
-        up, down = coarse_y(get, i, q, j)
-        right, left = z_beside(x)
+    place_coarse(2, cg, True)
+
+    for p, at_p, span in coarse_blocks(4):
+        here = pl.ds(0, span[1])
+        g = masked(cg[at_p, here, :], in_planes(p))
+        if in_planes(p) is not None:
+            cg[at_p, here, :] = g
+        update = g * (1.0 / THETA)
+        cxs[0, at_p, here, :] = update
+        cds[at_p, here, :] = update
+
+    def coarse_residual(now, at_p, span):
+        here = pl.ds(0, span[1])
+        x = cxs[now, at_p, here, :]
         return (
-            coarse_g(i, j, q) - x
-            + cw[0, i, j, q] * get(hi // CX, j, hi % CX)
-            + cw[1, i, j, q] * get(lo // CX, j, lo % CX)
-            + cw[2, i, j, q] * up
-            + cw[3, i, j, q] * down
-            + cw[4, i, j, q] * right
-            + cw[5, i, j, q] * left
+            cg[at_p, here, :]
+            - x
+            + spread(
+                x, lambda step, part: cxs[now, at_p + step, part[0] : part[1], :], span, CY,
+                lambda e: cw[e, at_p, here, :],
+            )
         )
 
     now = 0
-    for step, (first, second) in enumerate(cheb_terms()):
-        for plane, i, q, j in coarse_slots(3 - step):
-            update = first * cds[i, j, q] + second * coarse_residual(now, plane, i, q, j)
-            cds[i, j, q] = update
-            cxs[1 - now, i, j, q] = cxs[now, i, j, q] + update
+    for step, (first, second) in enumerate(terms):
+        for p, at_p, span in coarse_blocks(3 - step):
+            here = pl.ds(0, span[1])
+            update = first * cds[at_p, here, :] + second * coarse_residual(now, at_p, span)
+            cds[at_p, here, :] = update
+            cxs[1 - now, at_p, here, :] = cxs[now, at_p, here, :] + update
         now = 1 - now
 
     quarter = []
     for q in range(CX):
-        quarter.append(cdiag[q] * coarse_residual(now, q, 1, q, 1))
+        quarter.append(cdiag[q] * coarse_residual(now, CX + q, (0, CY)))
     for h in range(CX // 2):
         both = quarter[2 * h] + quarter[2 * h + 1]
         for t in range(2):
@@ -494,7 +516,7 @@
     ]
 
     for q in range(CX):
-        fine = double_z(cxs[now, 1, 1, q])
+        fine = double_z(cxs[now, CX + q, 0:CY])
         for t in range(4):
             part = fine[:, t * 128 : (t + 1) * 128]
             wide[t, pl.ds(0, CY, 2), :] = part
@@ -518,13 +540,15 @@
     dma = pltpu.SemaphoreType.DMA
     fine = (NX, NY, NZ)
     wide = (EX, EY, NZ)
+    coarse = (EXC, EYC, CZ)
     scratch = [
         vmem(wide, F32), vmem(wide, F32), vmem(wide, F32), vmem(wide, F32), vmem(wide, F32), vmem(wide, F32),
         vmem(wide, F32), vmem(fine, F32), vmem((6, *wide), F32),
         vmem((2, 18, 8, NZ), F32), vmem((2, 18, 8, NZ), F32), vmem((2, 2, 7, 8, NZ), F32),
         vmem((4, NY, 128), F32), vmem((4, NY, 128), F32),
-        vmem((3, 3, 2, CX, CY, CZ), F32), vmem((3, 3, CX, CY, CZ), F32), vmem((6, 3, 3, CX, CY, CZ), F32),
-        vmem((2, 3, 3, CX, CY, CZ), F32), vmem((3, 3, CX, CY, CZ), F32), vmem((CX, CY, CZ), F32),
+        vmem((2, *coarse), F32), vmem(coarse, F32), vmem((3, 2, CX // 2, 8, CZ), F32),
+        vmem((3, 3, 2, CX // 2, 8, CZ), F32), vmem((6, *coarse), F32),
+        vmem((2, *coarse), F32), vmem(coarse, F32), vmem((CX, CY, CZ), F32),
         vmem((8, 2, CY // 2, CZ // 2), F32),
         dma((4,)), dma((4, 2)), dma((4, 2)), dma((2,)), dma((2,)), dma((2, 2)), dma((2, 2)),
         dma((8,)), dma((8,)), dma((8,)), dma((8,)), dma((8,)), dma((8,)),

time: 36.9 us -> 34.5 us (0.935)
  Pallas kernels: 34.8 us -> 32.3 us
    pallas_call x1, Pallas kernels: 34.8 us -> 32.3 us  [on_device(): pl.pallas_call(kernel, out_shape=(jax.ShapeDtypeStruct(fine, F32), jax.Sh...]
where the time goes in v4:
time: 34.5 us; the launch traced here: 34.2 us
  Pallas kernels  32.3 us (94%)
  local copies, waits for them, and re-layouts  1.32 us (4%)
  between operations  0.64 us (2%)
    pallas_call x1, Pallas kernels, on_device(): pl.pallas_call(kernel, out_shape=(jax.ShapeDtypeStruct(fine, F32), jax.Sh...  32.3 us
    unnamed x2, local copies, waits for them, and re-layouts  1.32 us

profile of v4, /device:TPU:7, one launch (start us, length us, event | category | flops | bytes accessed | tf_op | source)
XLA Modules:
  0.0 34.2 jit_solution(16302756192286504667)
XLA Ops:
  0.6 32.3 %vcycle.1 = (f32[8,16,512]{2,1,0:T(8,128)S(1)}, f32[16,4,128]{2,1,0:T(4,128)S(1)}) custom-call(f32[8,16,512]{2,1,0:T(8,128)} %guess_h.1, f32[8,16,512]{2,1,0:T(8,128)} %rhs_h.1, f32[8,16,512]{2,1,0:T(8,128)} %alpha_h.1, f32[8,16,512]{2,1,0:T(8,128)} %beta_h.1), custom_call_target="tpu_custom_call" | custom-call | tf_op jit(solution)/shard_map/vcycle/pallas_call | solution.py:557
  32.9 0.7 %copy.8 = f32[8,16,512]{2,1,0:T(8,128)} copy(f32[8,16,512]{2,1,0:T(8,128)S(1)} %get-tuple-element.4) | data formatting | bytes 524288
  33.6 0.6 %copy.9 = f32[16,4,128]{2,1,0:T(4,128)} copy(f32[16,4,128]{2,1,0:T(4,128)S(1)} %get-tuple-element.5) | data formatting | bytes 65536

commit v5 on v4

--- a/solution.py
+++ b/solution.py
@@ -90,7 +90,7 @@
 
 def kernel(
     guess_h, rhs_h, alpha_h, beta_h, out_ref, last_ref,
-    xa, xb, be, al, rh, ds, gs, diag, ws, pk, rk, rc,
+    xa, xb, be, al, rh, ds, gs, diag, ws, pk, rk, qk, rc,
     pair, wide, cab, cg, pkc, rkc, cw, cxs, cds, cdiag, coarsest,
     load_sem, sx_sem, rx_sem, sy_sem, ry_sem, sc_sem, rc_sem, sab_sem, rab_sem, sg_sem, rg_sem, sl_sem, rl_sem,
 ):
@@ -113,23 +113,20 @@
     def greet(dx, dy):
         pl.semaphore_signal(barrier, inc=1, device_id=at(dx, dy), device_id_type=MESH)
 
+    own_x, own_y, edge_y = pl.ds(PX, NX), pl.ds(0, NY), pl.ds(NY, 8)
     around = [(dx, dy) for dx in (-1, 0, 1) for dy in (-1, 0, 1) if (dx, dy) != (0, 0)]
     barrier = pltpu.get_barrier_semaphore()
-    for dx in range(1, 8):
-        greet(dx, 0)
     for dx, dy in around:
         if dy != 0:
             when(beside[dy], functools.partial(greet, dx, dy))
-    greeted = 7 + 3 * (yz > 0).astype(jnp.int32) + 3 * (yz < nyz - 1).astype(jnp.int32)
-
-    own_x, own_y, edge_y = pl.ds(PX, NX), pl.ds(0, NY), pl.ds(NY, 8)
     loads = []
     for k, (src, dst) in enumerate(((guess_h, xa), (beta_h, be), (alpha_h, al), (rhs_h, rh))):
         copy = pltpu.make_async_copy(src, dst.at[own_x, own_y], load_sem.at[k])
         copy.start()
         loads.append(copy)
-    for copy in loads:
-        copy.wait()
+    for dx in range(1, 8):
+        greet(dx, 0)
+    greeted = 7 + 3 * (yz > 0).astype(jnp.int32) + 3 * (yz < nyz - 1).astype(jnp.int32)
 
     half = rows((8, NZ)) < 4
 
@@ -137,13 +134,20 @@
         moved = pltpu.roll(second, 4, 0)
         return jnp.where(half, moved, first) if side == 0 else jnp.where(half, first, moved)
 
-    for side, start, fifth in ((0, 8, 11), (1, 0, 4)):
-        tile = pl.ds(start, 8)
-        for p in range(NX):
-            pk[side, tile_a(p)] = packed(xa[PX + p, tile, :], be[PX + p, tile, :], side)
-            pk[side, tile_b(p)] = packed(al[PX + p, tile, :], rh[PX + p, tile, :], side)
-            pk[side, 16, p : p + 1, :] = xa[PX + p, fifth : fifth + 1, :]
-            pk[side, 17, p : p + 1, :] = be[PX + p, fifth : fifth + 1, :]
+    odd = lax.rem(gx, 2)
+
+    def pack_rows(half_at):
+        for side, start in ((0, 8), (1, 0)):
+            tile = pl.ds(start, 8)
+            for k in range(4):
+                p = 4 * half_at + k
+                one = PX + p
+                pk[side, 2 * p + half_at] = packed(xa[one, tile, :], be[one, tile, :], side)
+                pk[side, 2 * p + 1 - half_at] = packed(al[one, tile, :], rh[one, tile, :], side)
+
+    for copy in loads:
+        copy.wait()
+    pack_rows(odd)
     for side, missing in ((0, yz == 0), (1, yz == nyz - 1)):
 
         @pl.when(missing)
@@ -157,7 +161,7 @@
 
     pl.semaphore_wait(barrier, greeted)
 
-    sent, corners_sent = [], []
+    sent = []
 
     def copy_of(src, dst, s_sem, r_sem, device):
         return pltpu.make_async_remote_copy(
@@ -174,26 +178,18 @@
         for copy, dy in copies:
             when(beside[-dy], copy.wait_recv)
 
-    y_waits = [
-        send(pk.at[side], rk.at[side], sy_sem.at[side], ry_sem.at[side], 0, 1 - 2 * side) for side in (0, 1)
-    ]
     first_core = lax.rem(gx, 2) == 0
-    c_waits, relays = [], ([], [])
-    for sx in (0, 1):
-        part = pl.ds(9, 7) if sx == 0 else pl.ds(0, 7)
-        same_chip = first_core if sx == 0 else jnp.logical_not(first_core)
-        for sy in (0, 1):
-            dy = 1 - 2 * sy
-            sems = (sc_sem.at[sx, sy], rc_sem.at[sx, sy])
-            straight = copy_of(pk.at[sy, part], rc.at[sx, sy], *sems, at(1 - 2 * sx, dy))
-            relay = copy_of(rk.at[sy, part], rc.at[sx, sy], *sems, at(1 - 2 * sx, 0))
-            pl.when(jnp.logical_and(jnp.logical_not(same_chip), beside[dy]))(straight.start)
-            relays[sy].append((relay, jnp.logical_and(same_chip, beside[-dy])))
-            c_waits.append((straight, dy))
-            gone = jnp.logical_or(
-                jnp.logical_and(same_chip, beside[-dy]), jnp.logical_and(jnp.logical_not(same_chip), beside[dy])
-            )
-            corners_sent.append((straight, gone))
+    ahead = 8 * odd
+    parts = (pl.ds(ahead, 8), pl.ds(8 - ahead, 8), pl.ds(16, 2))
+
+    def send_rows(k):
+        part = parts[k]
+        return [
+            send(pk.at[side, part], rk.at[side, part], sy_sem.at[side, k], ry_sem.at[side, k], 0, 1 - 2 * side)
+            for side in (0, 1)
+        ]
+
+    y_waits = [send_rows(0)]
     x_waits = []
     for k, (src, dst, deep) in enumerate(
         ((guess_h, xa, DEPTH), (beta_h, be, DEPTH), (alpha_h, al, DEPTH - 1), (rhs_h, rh, DEPTH - 1))
@@ -210,6 +206,44 @@
                 sx_sem.at[k, 1], rx_sem.at[k, 1], -1, 0,
             )
         )
+
+    pack_rows(1 - odd)
+    y_waits.append(send_rows(1))
+    for side, fifth in ((0, 11), (1, 4)):
+        for p in range(NX):
+            pk[side, 16, p : p + 1, :] = xa[PX + p, fifth : fifth + 1, :]
+            pk[side, 17, p : p + 1, :] = be[PX + p, fifth : fifth + 1, :]
+    y_waits.append(send_rows(2))
+    sub = rows((8, NZ))
+    nearest = [(sub % 4) == 0, (sub % 4) == 3]
+    near_two = [(sub % 4) < 2, (sub % 4) >= 2]
+
+    def pack_corner(sx, sy):
+        planes = range(7, 3, -1) if sx == 0 else range(4)
+        a = [rk[sy, tile_a(p)] for p in planes]
+        b = [rk[sy, tile_b(p)] for p in planes]
+        one = 1 if sy == 0 else 7
+        qk[sx, sy, 0] = a[0]
+        qk[sx, sy, 1] = jnp.where(nearest[sy], pltpu.roll(a[3], one, 0), b[0])
+        qk[sx, sy, 2] = jnp.where(nearest[sy], pltpu.roll(b[2], one, 0), a[1])
+        qk[sx, sy, 3] = jnp.where(near_two[sy], pltpu.roll(a[2], 2, 0), b[1])
+
+    corners = []
+    for sx in (0, 1):
+        same_chip = first_core if sx == 0 else jnp.logical_not(first_core)
+        for sy in (0, 1):
+            relay = copy_of(qk.at[sx, sy], rc.at[sx, sy], sc_sem.at[sx, sy], rc_sem.at[sx, sy], at(1 - 2 * sx, 0))
+            corners.append((relay, beside[2 * sy - 1], sx, sy, same_chip))
+
+    def pass_on(side, on_chip):
+        for relay, arrives, sx, sy, same_chip in corners:
+            if sy == side:
+                chosen = same_chip if on_chip else jnp.logical_not(same_chip)
+
+                @pl.when(jnp.logical_and(arrives, chosen))
+                def _(relay=relay, sx=sx, sy=sy):
+                    pack_corner(sx, sy)
+                    relay.start()
 
     def restrict_pair(first, second):
         both = first + second
@@ -245,12 +279,6 @@
         cab[1, CX + q, 0:CY] = 0.125 * restrict_pair(be[one, own_y, :], be[two, own_y, :])
     for f in range(2):
         pack_coarse(f, lambda q, f=f: cab[f, CX + q, 0:CY])
-    slots = [pl.ds(k * CX, CX) for k in range(3)]
-    ab_waits = exchange_coarse(
-        pl.ds(0, 2), cab.at[:, slots[1], pl.ds(0, CY)],
-        [cab.at[:, slot, pl.ds(0, CY)] for slot in slots], sab_sem, rab_sem,
-    )
-
     in_lo_x = (gx > 0).astype(F32)
     in_hi_x = (gx < ngx - 1).astype(F32)
     in_lo_y = (yz > 0).astype(F32)
@@ -274,11 +302,19 @@
 
     def place_corners():
         for sx in (0, 1):
-            shift = 9 if sx == 0 else 0
-            for p in range(4, 8) if sx == 0 else range(4):
-                plane = PX + p - NX if sx == 0 else PX + p + NX
-                tiles = [tile_a(p) - shift] if p in (3, 4) else [tile_a(p) - shift, tile_b(p) - shift]
-                place(plane, *(rc[sx, side, tile] for tile in tiles for side in (0, 1)))
+            tiles = [[rc[sx, sy, k] for sy in (0, 1)] for k in range(4)]
+
+            def back(k):
+                return [pltpu.roll(tiles[k][0], 7, 0), pltpu.roll(tiles[k][1], 1, 0)]
+
+            blocks = (
+                [*tiles[0], *tiles[1]],
+                [*tiles[2], *tiles[3]],
+                [*(pltpu.roll(tile, 6, 0) for tile in tiles[3]), *back(2)],
+                back(1),
+            )
+            for k, block in enumerate(blocks):
+                place(PX - 1 - k if sx == 0 else PX + NX + k, *block)
         for edge, start in ((gx == 0, 0), (gx == ngx - 1, PX + NX)):
 
             @pl.when(edge)
@@ -438,14 +474,23 @@
                     later_step(step, p, span)
 
     for side in (0, 1):
-        wait_for(y_waits[side : side + 1])
-        for relay, passes in relays[side]:
-            pl.when(passes)(relay.start)
+        wait_for(y_waits[0][side : side + 1])
+        pass_on(side, False)
+    slots = [pl.ds(k * CX, CX) for k in range(3)]
+    ab_waits = exchange_coarse(
+        pl.ds(0, 2), cab.at[:, slots[1], pl.ds(0, CY)],
+        [cab.at[:, slot, pl.ds(0, CY)] for slot in slots], sab_sem, rab_sem,
+    )
+    for side in (0, 1):
+        wait_for(y_waits[1][side : side + 1])
+        pass_on(side, True)
+    wait_for(y_waits[2])
     place_rows()
     for step in range(DEGREE):
         fine_step(step, True)
     wait_for(x_waits)
-    wait_for(c_waits)
+    for relay, arrives, *_ in corners:
+        pl.when(arrives)(relay.wait_recv)
     place_corners()
     for step in range(DEGREE):
         fine_step(step, False)
@@ -531,8 +576,8 @@
         last_ref[pl.ds(2 * owner, 2)] = coarsest[dx]
     for copy, dy in sent:
         when(beside[dy], copy.wait_send)
-    for copy, gone in corners_sent:
-        pl.when(gone)(copy.wait_send)
+    for relay, arrives, *_ in corners:
+        pl.when(arrives)(relay.wait_send)
 
 
 def on_device(guess, rhs, alpha, beta):
@@ -544,13 +589,13 @@
     scratch = [
         vmem(wide, F32), vmem(wide, F32), vmem(wide, F32), vmem(wide, F32), vmem(wide, F32), vmem(wide, F32),
         vmem(wide, F32), vmem(fine, F32), vmem((6, *wide), F32),
-        vmem((2, 18, 8, NZ), F32), vmem((2, 18, 8, NZ), F32), vmem((2, 2, 7, 8, NZ), F32),
+        vmem((2, 18, 8, NZ), F32), vmem((2, 18, 8, NZ), F32), vmem((2, 2, 4, 8, NZ), F32), vmem((2, 2, 4, 8, NZ), F32),
         vmem((4, NY, 128), F32), vmem((4, NY, 128), F32),
         vmem((2, *coarse), F32), vmem(coarse, F32), vmem((3, 2, CX // 2, 8, CZ), F32),
         vmem((3, 3, 2, CX // 2, 8, CZ), F32), vmem((6, *coarse), F32),
         vmem((2, *coarse), F32), vmem(coarse, F32), vmem((CX, CY, CZ), F32),
         vmem((8, 2, CY // 2, CZ // 2), F32),
-        dma((4,)), dma((4, 2)), dma((4, 2)), dma((2,)), dma((2,)), dma((2, 2)), dma((2, 2)),
+        dma((4,)), dma((4, 2)), dma((4, 2)), dma((2, 3)), dma((2, 3)), dma((2, 2)), dma((2, 2)),
         dma((8,)), dma((8,)), dma((8,)), dma((8,)), dma((8,)), dma((8,)),
     ]
     placed = [pltpu.with_memory_space_constraint(x, pltpu.HBM) for x in (guess, rhs, alpha, beta)]

time: 34.5 us -> 32.7 us (0.948)
  Pallas kernels: 32.3 us -> 30.3 us
    pallas_call x1, Pallas kernels: 32.3 us -> 30.3 us  [on_device(): pl.pallas_call(kernel, out_shape=(jax.ShapeDtypeStruct(fine, F32), jax.Sh...]
where the time goes in v5:
time: 32.7 us; the launch traced here: 32.3 us
  Pallas kernels  30.3 us (93%)
  local copies, waits for them, and re-layouts  1.32 us (4%)
  between operations  0.64 us (2%)
    pallas_call x1, Pallas kernels, on_device(): pl.pallas_call(kernel, out_shape=(jax.ShapeDtypeStruct(fine, F32), jax.Sh...  30.3 us
    unnamed x2, local copies, waits for them, and re-layouts  1.32 us

profile of v5, /device:TPU:7, one launch (start us, length us, event | category | flops | bytes accessed | tf_op | source)
XLA Modules:
  0.0 32.3 jit_solution(454728371837759703)
XLA Ops:
  0.6 30.3 %vcycle.1 = (f32[8,16,512]{2,1,0:T(8,128)S(1)}, f32[16,4,128]{2,1,0:T(4,128)S(1)}) custom-call(f32[8,16,512]{2,1,0:T(8,128)} %guess_h.1, f32[8,16,512]{2,1,0:T(8,128)} %rhs_h.1, f32[8,16,512]{2,1,0:T(8,128)} %alpha_h.1, f32[8,16,512]{2,1,0:T(8,128)} %beta_h.1), custom_call_target="tpu_custom_call" | custom-call | tf_op jit(solution)/shard_map/vcycle/pallas_call | solution.py:602
  31.0 0.7 %copy.8 = f32[8,16,512]{2,1,0:T(8,128)} copy(f32[8,16,512]{2,1,0:T(8,128)S(1)} %get-tuple-element.4) | data formatting | bytes 524288
  31.7 0.6 %copy.9 = f32[16,4,128]{2,1,0:T(4,128)} copy(f32[16,4,128]{2,1,0:T(4,128)S(1)} %get-tuple-element.5) | data formatting | bytes 65536

commit v6 on v5

--- a/solution.py
+++ b/solution.py
@@ -67,6 +67,17 @@
     return jnp.concatenate(tiles, axis=1)
 
 
+def without_last(field):
+    width = field.shape[1]
+    tail = field[:, width - 128 :]
+    return jnp.concatenate([field[:, : width - 128], jnp.where(lanes(tail.shape) == 127, 0.0, tail)], axis=1)
+
+
+def without_first(field):
+    head = field[:, :128]
+    return jnp.concatenate([jnp.where(lanes(head.shape) == 0, 0.0, head), field[:, 128:]], axis=1)
+
+
 def z_beside(field):
     width = field.shape[1]
     return pltpu.roll(field, width - 1, 1), pltpu.roll(field, 1, 1)
@@ -114,7 +125,7 @@
         pl.semaphore_signal(barrier, inc=1, device_id=at(dx, dy), device_id_type=MESH)
 
     own_x, own_y, edge_y = pl.ds(PX, NX), pl.ds(0, NY), pl.ds(NY, 8)
-    around = [(dx, dy) for dx in (-1, 0, 1) for dy in (-1, 0, 1) if (dx, dy) != (0, 0)]
+    around = [(-1, -1), (-1, 1), (1, -1), (1, 1), (0, -1), (0, 1), (-1, 0), (1, 0)]
     barrier = pltpu.get_barrier_semaphore()
     for dx, dy in around:
         if dy != 0:
@@ -348,15 +359,14 @@
             w(0) * x_at(1, span) + w(1) * x_at(-1, span) + w(2) * up + w(3) * down + w(4) * right + w(5) * left
         )
 
-    def in_rows(shape, own):
-        row = rows(shape)
-        return jnp.where(row < own, 1.0, jnp.where(row < own + 4, in_hi_y, in_lo_y))
+    def in_rows(value, own):
+        tail = value[own:]
+        inside = jnp.where(rows(tail.shape) < 4, in_hi_y, in_lo_y)
+        return jnp.concatenate([value[:own], tail * inside], axis=0)
 
     def first_step(p, span):
         lo, hi = span
         here = pl.ds(lo, hi - lo)
-        shape = (hi - lo, NZ)
-        lane = lanes(shape)
         b = be[PX + p, here, :]
         fifth = fifth_b = None
         if 0 <= p < NX:
@@ -365,14 +375,13 @@
             fifth_b = (rk[0, 17, part, :] * in_lo_y, rk[1, 17, part, :] * in_hi_y)
         b_up, b_down = along_y(b, lambda row: be[PX + p, row : row + 1, :], span, NY, fifth_b)
         b_right, b_left = z_beside(b)
-        b_right = jnp.where(lane == NZ - 1, 0.0, b_right)
-        b_left = jnp.where(lane == 0, 0.0, b_left)
-        faces = [
-            0.5 * (b + other)
-            for other in (be[PX + p + 1, here, :], be[PX + p - 1, here, :], b_up, b_down, b_right, b_left)
+        b_right = without_last(b_right)
+        b_left = without_first(b_left)
+        pairs = [
+            b + other for other in (be[PX + p + 1, here, :], be[PX + p - 1, here, :], b_up, b_down, b_right, b_left)
         ]
-        total = faces[0] + faces[1] + faces[2] + faces[3] + faces[4] + faces[5]
-        whole = al[PX + p, here, :] + total
+        total = pairs[0] + pairs[1] + pairs[2] + pairs[3] + pairs[4] + pairs[5]
+        whole = al[PX + p, here, :] + 0.5 * total
         if 0 <= p < NX:
             diag[p] = whole[0:NY]
         inverse = 1.0 / whole
@@ -381,10 +390,11 @@
         if p >= NX:
             inverse = inverse * in_hi_x
         if span == (0, EY):
-            inverse = inverse * in_rows(shape, NY)
-        w = [inverse * face for face in faces]
-        w[4] = jnp.where(lane == NZ - 1, 0.0, w[4])
-        w[5] = jnp.where(lane == 0, 0.0, w[5])
+            inverse = in_rows(inverse, NY)
+        scale = 0.5 * inverse
+        w = [scale * pair for pair in pairs]
+        w[4] = without_last(w[4])
+        w[5] = without_first(w[5])
         for e in range(6):
             ws[e, PX + p, here, :] = w[e]
         g = inverse * rh[PX + p, here, :]
@@ -420,8 +430,8 @@
     def masked(value, mask):
         return value if mask is None else value * mask
 
-    def place_coarse(f, field, inside):
-        for k in range(3):
+    def place_coarse(f, field, inside, slots=(0, 1, 2)):
+        for k in slots:
             for q in range(0, CX, 2):
                 below, above = rkc[f, k, 0, q // 2], rkc[f, k, 1, q // 2]
                 if inside:
@@ -432,13 +442,11 @@
     def coarse_setup(own_only):
         for p, at_p, span in coarse_blocks(0 if own_only else 3):
             here = pl.ds(0, span[1])
-            shape = (span[1], CZ)
-            clane = lanes(shape)
             b = cab[1, at_p, here, :]
             b_up, b_down = along_y(b, lambda row: cab[1, at_p, row : row + 1, :], span, CY)
             b_right, b_left = z_beside(b)
-            b_right = jnp.where(clane == CZ - 1, 0.0, b_right)
-            b_left = jnp.where(clane == 0, 0.0, b_left)
+            b_right = without_last(b_right)
+            b_left = without_first(b_left)
             faces = [
                 0.5 * (b + other)
                 for other in (cab[1, at_p + 1, here, :], cab[1, at_p - 1, here, :], b_up, b_down, b_right, b_left)
@@ -450,10 +458,10 @@
                 continue
             scale = masked(0.25 / whole, in_planes(p))
             if span == (0, EYC):
-                scale = scale * in_rows(shape, CY)
+                scale = in_rows(scale, CY)
             w = [scale * face for face in faces]
-            w[4] = jnp.where(clane == CZ - 1, 0.0, w[4])
-            w[5] = jnp.where(clane == 0, 0.0, w[5])
+            w[4] = without_last(w[4])
+            w[5] = without_first(w[5])
             for e in range(6):
                 cw[e, at_p, here, :] = w[e]
 
@@ -497,10 +505,9 @@
     cur = xa if DEGREE % 2 == 0 else xb
     own = (0, NY)
     wait_for(ab_waits)
-    place_coarse(0, cab.at[0], False)
-    place_coarse(1, cab.at[1], True)
-    for p in (*range(-CX, 0), *range(CX, 2 * CX)):
-        cab[1, CX + p] = cab[1, CX + p] * in_planes(p)
+    place_coarse(1, cab.at[1], True, (1,))
+    for p in (-1, CX):
+        cab[1, CX + p, 0:CY] = cab[1, CX + p, 0:CY] * in_planes(p)
     coarse_setup(True)
     for q in range(CX):
         a = diag[2 * q] * residual(cur, 2 * q, own)
@@ -511,6 +518,10 @@
     g_waits = exchange_coarse(
         2, cg.at[slots[1], pl.ds(0, CY)], [cg.at[slot, pl.ds(0, CY)] for slot in slots], sg_sem, rg_sem
     )
+    place_coarse(0, cab.at[0], False)
+    place_coarse(1, cab.at[1], True, (0, 2))
+    for p in (*range(-CX, 0), *range(CX, 2 * CX)):
+        cab[1, CX + p] = cab[1, CX + p] * in_planes(p)
     coarse_setup(False)
     wait_for(g_waits)
     place_coarse(2, cg, True)
@@ -557,7 +568,7 @@
         )
         coarsest[0, h] = 0.125 * halve_z(summed)
     l_waits = [
-        send(coarsest.at[0], coarsest.at[dx], sl_sem.at[dx], rl_sem.at[dx], dx, 0) for dx in range(1, 8)
+        send(coarsest.at[0], coarsest.at[dx], sl_sem.at[dx], rl_sem.at[dx], dx, 0) for dx in (4, 5, 3, 6, 2, 7, 1)
     ]
 
     for q in range(CX):
@@ -578,6 +589,14 @@
         when(beside[dy], copy.wait_send)
     for relay, arrives, *_ in corners:
         pl.when(arrives)(relay.wait_send)
+
+
+def store(field, last, field_out, last_out, sem):
+    copies = [pltpu.make_async_copy(field, field_out, sem.at[0]), pltpu.make_async_copy(last, last_out, sem.at[1])]
+    for copy in copies:
+        copy.start()
+    for copy in copies:
+        copy.wait()
 
 
 def on_device(guess, rhs, alpha, beta):
@@ -599,7 +618,7 @@
         dma((8,)), dma((8,)), dma((8,)), dma((8,)), dma((8,)), dma((8,)),
     ]
     placed = [pltpu.with_memory_space_constraint(x, pltpu.HBM) for x in (guess, rhs, alpha, beta)]
-    return pl.pallas_call(
+    results = pl.pallas_call(
         kernel,
         out_shape=(
             jax.ShapeDtypeStruct(fine, F32),
@@ -613,6 +632,18 @@
         ),
         name="vcycle",
     )(*placed)
+    return pl.pallas_call(
+        store,
+        out_shape=(
+            jax.ShapeDtypeStruct(fine, F32),
+            jax.ShapeDtypeStruct((16, CY // 2, CZ // 2), F32),
+        ),
+        in_specs=[pl.BlockSpec(memory_space=vmem)] * 2,
+        out_specs=(pl.BlockSpec(memory_space=pltpu.HBM), pl.BlockSpec(memory_space=pltpu.HBM)),
+        scratch_shapes=[dma((2,))],
+        compiler_params=pltpu.CompilerParams(vmem_limit_bytes=4 << 20),
+        name="store",
+    )(*results)
 
 
 def solution(mesh):

time: 32.7 us -> 31.8 us (0.972)
  local copies, waits for them, and re-layouts: 1.32 us -> 0 us
  Pallas kernels: 30.3 us -> 31 us
    unnamed x2 -> x0, local copies, waits for them, and re-layouts: 1.32 us -> none
    pallas_call x0 -> x1, Pallas kernels: none -> 0.72 us  [on_device(): pl.pallas_call(store, out_shape=(jax.ShapeDtypeStruct(fine, F32), jax.Sha...]
where the time goes in v6:
time: 31.8 us; the launch traced here: 31.7 us
  Pallas kernels  31 us (97%)
  between operations  0.64 us (2%)
    pallas_call x1, Pallas kernels, on_device(): pl.pallas_call(kernel, out_shape=(jax.ShapeDtypeStruct(fine, F32), jax.Sh...  30.3 us
    pallas_call x1, Pallas kernels, on_device(): pl.pallas_call(store, out_shape=(jax.ShapeDtypeStruct(fine, F32), jax.Sha...  0.72 us

profile of v6, /device:TPU:7, one launch (start us, length us, event | category | flops | bytes accessed | tf_op | source)
XLA Modules:
  0.0 31.7 jit_solution(2023964426575642628)
XLA Ops:
  0.6 30.3 %vcycle.1 = (f32[8,16,512]{2,1,0:T(8,128)S(1)}, f32[16,4,128]{2,1,0:T(4,128)S(1)}) custom-call(f32[8,16,512]{2,1,0:T(8,128)} %guess_h.1, f32[8,16,512]{2,1,0:T(8,128)} %rhs_h.1, f32[8,16,512]{2,1,0:T(8,128)} %alpha_h.1, f32[8,16,512]{2,1,0:T(8,128)} %beta_h.1), custom_call_target="tpu_custom_call" | custom-call | tf_op jit(solution)/shard_map/vcycle/pallas_call | solution.py:621
  30.9 0.7 %store.1 = (f32[8,16,512]{2,1,0:T(8,128)}, f32[16,4,128]{2,1,0:T(4,128)}) custom-call(f32[8,16,512]{2,1,0:T(8,128)S(1)} %get-tuple-element.4.field, f32[16,4,128]{2,1,0:T(4,128)S(1)} %get-tuple-element.5.last), custom_call_target="tpu_custom_call" | custom-call | tf_op jit(solution)/shard_map/store/pallas_call | solution.py:635

commit v7 on v6

--- a/solution.py
+++ b/solution.py
@@ -102,7 +102,7 @@
 def kernel(
     guess_h, rhs_h, alpha_h, beta_h, out_ref, last_ref,
     xa, xb, be, al, rh, ds, gs, diag, ws, pk, rk, qk, rc,
-    pair, wide, cab, cg, pkc, rkc, cw, cxs, cds, cdiag, coarsest,
+    pair, wide, cab, cg, pkc, rkc, pcc, rcc, cw, cxs, cds, cdiag, coarsest,
     load_sem, sx_sem, rx_sem, sy_sem, ry_sem, sc_sem, rc_sem, sab_sem, rab_sem, sg_sem, rg_sem, sl_sem, rl_sem,
 ):
     gx = lax.axis_index("gx")
@@ -167,8 +167,9 @@
             for k in range(3):
                 if k < 2:
                     rc[k, side] = jnp.ones(rc.shape[2:], F32)
-                for f in range(3):
-                    rkc[f, k, side] = jnp.ones(rkc.shape[3:], F32)
+                    for f in range(3):
+                        rcc[f, k, side] = jnp.ones(rcc.shape[3:], F32)
+                rkc[k, side] = jnp.ones(rkc.shape[2:], F32)
 
     pl.semaphore_wait(barrier, greeted)
 
@@ -265,13 +266,20 @@
         )
         return halve_z(summed)
 
-    chalf = rows((8, CZ)) < 4
+    csub = rows((8, CZ))
+    chalf = csub < 4
 
     def pack_coarse(f, get):
         for q in range(0, CX, 2):
             this, then = get(q), pltpu.roll(get(q + 1), 4, 0)
             pkc[f, 0, q // 2] = jnp.where(chalf, then, this)
             pkc[f, 1, q // 2] = jnp.where(chalf, this, then)
+        for ix, (tile, third, slots_at) in enumerate(((1, 1, (4, 3)), (0, 2, (0, 7)))):
+            near = get(third)
+            for side, row in ((0, near[CY - 1 : CY]), (1, near[0:1])):
+                pcc[f, ix, side] = jnp.where(
+                    csub == slots_at[side], jnp.broadcast_to(row, (8, CZ)), pkc[f, side, tile]
+                )
 
     def exchange_coarse(fields, own, others, s_sem, r_sem):
         copies = []
@@ -280,7 +288,11 @@
                 src, dst = own, others[1 - dx]
             else:
                 side = (1 - dy) // 2
-                src, dst = pkc.at[fields, side], rkc.at[fields, 1 - dx, side]
+                if dx == 0:
+                    src, dst = pkc.at[fields, side], rkc.at[fields, side]
+                else:
+                    ix = (1 - dx) // 2
+                    src, dst = pcc.at[fields, ix, side], rcc.at[fields, ix, side]
             copies.append(send(src, dst, s_sem.at[k], r_sem.at[k], dx, dy))
         return copies
 
@@ -431,13 +443,27 @@
         return value if mask is None else value * mask
 
     def place_coarse(f, field, inside, slots=(0, 1, 2)):
+        def inner(below, above):
+            return (below * in_lo_y, above * in_hi_y) if inside else (below, above)
+
+        def join_rows(plane, below, above):
+            field[plane, pl.ds(CY, 8), :] = jnp.where(chalf, above, below)
+            field[plane + 1, pl.ds(CY, 8), :] = pltpu.roll(jnp.where(chalf, below, above), 4, 0)
+
         for k in slots:
-            for q in range(0, CX, 2):
-                below, above = rkc[f, k, 0, q // 2], rkc[f, k, 1, q // 2]
-                if inside:
-                    below, above = below * in_lo_y, above * in_hi_y
-                field[k * CX + q, pl.ds(CY, 8), :] = jnp.where(chalf, above, below)
-                field[k * CX + q + 1, pl.ds(CY, 8), :] = pltpu.roll(jnp.where(chalf, below, above), 4, 0)
+            if k == 1:
+                for q in range(0, CX, 2):
+                    join_rows(CX + q, *inner(rkc[f, 0, q // 2], rkc[f, 1, q // 2]))
+                continue
+            ix = k // 2
+            below, above = inner(rcc[f, ix, 0], rcc[f, ix, 1])
+            join_rows(2 if ix == 0 else 2 * CX, below, above)
+            low, high = (4, 3) if ix == 0 else (0, 7)
+            field[1 if ix == 0 else 2 * CX + 2, pl.ds(CY, 8), :] = jnp.where(
+                chalf,
+                jnp.broadcast_to(above[high : high + 1], (8, CZ)),
+                jnp.broadcast_to(below[low : low + 1], (8, CZ)),
+            )
 
     def coarse_setup(own_only):
         for p, at_p, span in coarse_blocks(0 if own_only else 3):
@@ -567,6 +593,7 @@
             [pair[t, pl.ds(0, CY // 2, 2), :] + pair[t, pl.ds(1, CY // 2, 2), :] for t in range(2)], axis=1
         )
         coarsest[0, h] = 0.125 * halve_z(summed)
+    earlier = len(sent)
     l_waits = [
         send(coarsest.at[0], coarsest.at[dx], sl_sem.at[dx], rl_sem.at[dx], dx, 0) for dx in (4, 5, 3, 6, 2, 7, 1)
     ]
@@ -581,14 +608,16 @@
         for p in (2 * q, 2 * q + 1):
             out_ref[p] = cur[PX + p, own_y, :] + full
 
+    for copy, dy in sent[:earlier]:
+        when(beside[dy], copy.wait_send)
+    for relay, arrives, *_ in corners:
+        pl.when(arrives)(relay.wait_send)
     wait_for(l_waits)
     for dx in range(8):
         owner = lax.rem(gx + ngx - dx, ngx)
         last_ref[pl.ds(2 * owner, 2)] = coarsest[dx]
-    for copy, dy in sent:
-        when(beside[dy], copy.wait_send)
-    for relay, arrives, *_ in corners:
-        pl.when(arrives)(relay.wait_send)
+    for copy, _ in l_waits:
+        copy.wait_send()
 
 
 def store(field, last, field_out, last_out, sem):
@@ -611,7 +640,8 @@
         vmem((2, 18, 8, NZ), F32), vmem((2, 18, 8, NZ), F32), vmem((2, 2, 4, 8, NZ), F32), vmem((2, 2, 4, 8, NZ), F32),
         vmem((4, NY, 128), F32), vmem((4, NY, 128), F32),
         vmem((2, *coarse), F32), vmem(coarse, F32), vmem((3, 2, CX // 2, 8, CZ), F32),
-        vmem((3, 3, 2, CX // 2, 8, CZ), F32), vmem((6, *coarse), F32),
+        vmem((3, 2, CX // 2, 8, CZ), F32), vmem((3, 2, 2, 8, CZ), F32), vmem((3, 2, 2, 8, CZ), F32),
+        vmem((6, *coarse), F32),
         vmem((2, *coarse), F32), vmem(coarse, F32), vmem((CX, CY, CZ), F32),
         vmem((8, 2, CY // 2, CZ // 2), F32),
         dma((4,)), dma((4, 2)), dma((4, 2)), dma((2, 3)), dma((2, 3)), dma((2, 2)), dma((2, 2)),

time: 31.8 us -> 31.6 us (level)
  no operation moved by 1% of the time
where the time goes in v7:
time: 31.6 us; the launch traced here: 31.4 us
  Pallas kernels  30.8 us (97%)
  between operations  0.64 us (2%)
    pallas_call x1, Pallas kernels, on_device(): pl.pallas_call(kernel, out_shape=(jax.ShapeDtypeStruct(fine, F32), jax.Sh...  30.1 us
    pallas_call x1, Pallas kernels, on_device(): pl.pallas_call(store, out_shape=(jax.ShapeDtypeStruct(fine, F32), jax.Sha...  0.72 us

profile of v7, /device:TPU:7, one launch (start us, length us, event | category | flops | bytes accessed | tf_op | source)
XLA Modules:
  0.0 31.4 jit_solution(6528077225647206830)
XLA Ops:
  0.6 30.1 %vcycle.1 = (f32[8,16,512]{2,1,0:T(8,128)S(1)}, f32[16,4,128]{2,1,0:T(4,128)S(1)}) custom-call(f32[8,16,512]{2,1,0:T(8,128)} %guess_h.1, f32[8,16,512]{2,1,0:T(8,128)} %rhs_h.1, f32[8,16,512]{2,1,0:T(8,128)} %alpha_h.1, f32[8,16,512]{2,1,0:T(8,128)} %beta_h.1), custom_call_target="tpu_custom_call" | custom-call | tf_op jit(solution)/shard_map/vcycle/pallas_call | solution.py:651
  30.7 0.7 %store.1 = (f32[8,16,512]{2,1,0:T(8,128)}, f32[16,4,128]{2,1,0:T(4,128)}) custom-call(f32[8,16,512]{2,1,0:T(8,128)S(1)} %get-tuple-element.4.field, f32[16,4,128]{2,1,0:T(4,128)S(1)} %get-tuple-element.5.last), custom_call_target="tpu_custom_call" | custom-call | tf_op jit(solution)/shard_map/store/pallas_call | solution.py:665

commit v8 on v7

--- a/solution.py
+++ b/solution.py
@@ -323,6 +323,15 @@
         for p in range(NX):
             place(PX + p, rk[0, tile_a(p)], rk[1, tile_a(p)], rk[0, tile_b(p)], rk[1, tile_b(p)])
 
+    def fill_edges():
+        for edge, start in ((gx == 0, 0), (gx == ngx - 1, PX + NX)):
+
+            @pl.when(edge)
+            def _(start=start):
+                for plane in range(start, start + DEPTH):
+                    xa[plane] = jnp.zeros((EY, NZ), F32)
+                    be[plane] = jnp.zeros((EY, NZ), F32)
+
     def place_corners():
         for sx in (0, 1):
             tiles = [[rc[sx, sy, k] for sy in (0, 1)] for k in range(4)]
@@ -338,13 +347,7 @@
             )
             for k, block in enumerate(blocks):
                 place(PX - 1 - k if sx == 0 else PX + NX + k, *block)
-        for edge, start in ((gx == 0, 0), (gx == ngx - 1, PX + NX)):
-
-            @pl.when(edge)
-            def _(start=start):
-                for plane in range(start, start + DEPTH):
-                    xa[plane] = jnp.zeros((EY, NZ), F32)
-                    be[plane] = jnp.zeros((EY, NZ), F32)
+        fill_edges()
 
     def fine_blocks(deep):
         found = []
@@ -357,6 +360,13 @@
         count = own + 8
         if span == (0, own):
             return y_beside(x, at_row(count - 1), at_row(own))
+        if span == (own, count):
+            up, down = y_beside(x, at_row(own - 1), at_row(0))
+            if fifth is not None:
+                row = rows(x.shape)
+                up = jnp.where(row == 3, jnp.broadcast_to(fifth[1], x.shape), up)
+                down = jnp.where(row == 4, jnp.broadcast_to(fifth[0], x.shape), down)
+            return up, down
         up, down = pltpu.roll(x, count - 1, 0), pltpu.roll(x, 1, 0)
         if fifth is not None:
             row = rows(x.shape)
@@ -394,7 +404,7 @@
         ]
         total = pairs[0] + pairs[1] + pairs[2] + pairs[3] + pairs[4] + pairs[5]
         whole = al[PX + p, here, :] + 0.5 * total
-        if 0 <= p < NX:
+        if 0 <= p < NX and lo == 0:
             diag[p] = whole[0:NY]
         inverse = 1.0 / whole
         if p < 0:
@@ -403,6 +413,8 @@
             inverse = inverse * in_hi_x
         if span == (0, EY):
             inverse = in_rows(inverse, NY)
+        if span == (NY, EY):
+            inverse = inverse * jnp.where(rows(inverse.shape) < 4, in_hi_y, in_lo_y)
         scale = 0.5 * inverse
         w = [scale * pair for pair in pairs]
         w[4] = without_last(w[4])
@@ -502,10 +514,7 @@
     def fine_step(step, chosen):
         for p, span in fine_blocks(DEPTH - 1 - step):
             if (1 + step <= p < NX - 1 - step) == chosen:
-                if step == 0:
-                    first_step(p, span)
-                else:
-                    later_step(step, p, span)
+                later_step(step, p, span)
 
     for side in (0, 1):
         wait_for(y_waits[0][side : side + 1])
@@ -518,15 +527,25 @@
     for side in (0, 1):
         wait_for(y_waits[1][side : side + 1])
         pass_on(side, True)
+    place_rows()
+    wait_for(x_waits)
+    fill_edges()
+    for p in range(NX):
+        first_step(p, (0, NY))
     wait_for(y_waits[2])
-    place_rows()
-    for step in range(DEGREE):
+    for p in range(1, NX - 1):
+        first_step(p, (NY, EY))
+    for step in range(1, DEGREE):
         fine_step(step, True)
-    wait_for(x_waits)
     for relay, arrives, *_ in corners:
         pl.when(arrives)(relay.wait_recv)
     place_corners()
-    for step in range(DEGREE):
+    for p, span in fine_blocks(DEPTH - 1):
+        if not 0 <= p < NX:
+            first_step(p, span)
+        elif p in (0, NX - 1):
+            first_step(p, (NY, EY))
+    for step in range(1, DEGREE):
         fine_step(step, False)
     cur = xa if DEGREE % 2 == 0 else xb
     own = (0, NY)

time: 31.6 us -> 31 us (0.981)
  Pallas kernels: 30.8 us -> 30.2 us
    pallas_call x1, Pallas kernels: 30.1 us -> 29.5 us  [on_device(): pl.pallas_call(kernel, out_shape=(jax.ShapeDtypeStruct(fine, F32), jax.Sh...]
where the time goes in v8:
time: 31 us; the launch traced here: 30.9 us
  Pallas kernels  30.2 us (97%)
  between operations  0.64 us (2%)
    pallas_call x1, Pallas kernels, on_device(): pl.pallas_call(kernel, out_shape=(jax.ShapeDtypeStruct(fine, F32), jax.Sh...  29.5 us
    pallas_call x1, Pallas kernels, on_device(): pl.pallas_call(store, out_shape=(jax.ShapeDtypeStruct(fine, F32), jax.Sha...  0.72 us

profile of v8, /device:TPU:7, one launch (start us, length us, event | category | flops | bytes accessed | tf_op | source)
XLA Modules:
  0.0 30.9 jit_solution(6025203788160712214)
XLA Ops:
  0.6 29.5 %vcycle.1 = (f32[8,16,512]{2,1,0:T(8,128)S(1)}, f32[16,4,128]{2,1,0:T(4,128)S(1)}) custom-call(f32[8,16,512]{2,1,0:T(8,128)} %guess_h.1, f32[8,16,512]{2,1,0:T(8,128)} %rhs_h.1, f32[8,16,512]{2,1,0:T(8,128)} %alpha_h.1, f32[8,16,512]{2,1,0:T(8,128)} %beta_h.1), custom_call_target="tpu_custom_call" | custom-call | tf_op jit(solution)/shard_map/vcycle/pallas_call | solution.py:670
  30.2 0.7 %store.1 = (f32[8,16,512]{2,1,0:T(8,128)}, f32[16,4,128]{2,1,0:T(4,128)}) custom-call(f32[8,16,512]{2,1,0:T(8,128)S(1)} %get-tuple-element.4.field, f32[16,4,128]{2,1,0:T(4,128)S(1)} %get-tuple-element.5.last), custom_call_target="tpu_custom_call" | custom-call | tf_op jit(solution)/shard_map/store/pallas_call | solution.py:684

commit v9 on v8

--- a/solution.py
+++ b/solution.py
@@ -513,7 +513,9 @@
 
     def fine_step(step, chosen):
         for p, span in fine_blocks(DEPTH - 1 - step):
-            if (1 + step <= p < NX - 1 - step) == chosen:
+            if p in (step, NX - 1 - step):
+                later_step(step, p, (0, NY) if chosen else (NY, EY))
+            elif (step < p < NX - 1 - step) == chosen:
                 later_step(step, p, span)
 
     for side in (0, 1):
@@ -549,7 +551,7 @@
         fine_step(step, False)
     cur = xa if DEGREE % 2 == 0 else xb
     own = (0, NY)
-    wait_for(ab_waits)
+    wait_for(ab_waits[4:])
     place_coarse(1, cab.at[1], True, (1,))
     for p in (-1, CX):
         cab[1, CX + p, 0:CY] = cab[1, CX + p, 0:CY] * in_planes(p)
@@ -563,6 +565,7 @@
     g_waits = exchange_coarse(
         2, cg.at[slots[1], pl.ds(0, CY)], [cg.at[slot, pl.ds(0, CY)] for slot in slots], sg_sem, rg_sem
     )
+    wait_for(ab_waits[:4])
     place_coarse(0, cab.at[0], False)
     place_coarse(1, cab.at[1], True, (0, 2))
     for p in (*range(-CX, 0), *range(CX, 2 * CX)):

time: 31 us -> 31 us (level)
  no operation moved by 1% of the time
where the time goes in v9:
time: 31 us; the launch traced here: 30.9 us
  Pallas kernels  30.2 us (97%)
  between operations  0.64 us (2%)
    pallas_call x1, Pallas kernels, on_device(): pl.pallas_call(kernel, out_shape=(jax.ShapeDtypeStruct(fine, F32), jax.Sh...  29.5 us
    pallas_call x1, Pallas kernels, on_device(): pl.pallas_call(store, out_shape=(jax.ShapeDtypeStruct(fine, F32), jax.Sha...  0.72 us

profile of v9, /device:TPU:7, one launch (start us, length us, event | category | flops | bytes accessed | tf_op | source)
XLA Modules:
  0.0 30.9 jit_solution(12428516278444780213)
XLA Ops:
  0.6 29.5 %vcycle.1 = (f32[8,16,512]{2,1,0:T(8,128)S(1)}, f32[16,4,128]{2,1,0:T(4,128)S(1)}) custom-call(f32[8,16,512]{2,1,0:T(8,128)} %guess_h.1, f32[8,16,512]{2,1,0:T(8,128)} %rhs_h.1, f32[8,16,512]{2,1,0:T(8,128)} %alpha_h.1, f32[8,16,512]{2,1,0:T(8,128)} %beta_h.1), custom_call_target="tpu_custom_call" | custom-call | tf_op jit(solution)/shard_map/vcycle/pallas_call | solution.py:673
  30.1 0.7 %store.1 = (f32[8,16,512]{2,1,0:T(8,128)}, f32[16,4,128]{2,1,0:T(4,128)}) custom-call(f32[8,16,512]{2,1,0:T(8,128)S(1)} %get-tuple-element.4.field, f32[16,4,128]{2,1,0:T(4,128)S(1)} %get-tuple-element.5.last), custom_call_target="tpu_custom_call" | custom-call | tf_op jit(solution)/shard_map/store/pallas_call | solution.py:687
